TPU v7x, 128 devices: a whole 4x4x4 slice. The times are simulated.
128 devices in a mesh: dp: 8 (over z, x_hi), ctx: 16 (over x_lo, y, core).
Axes of the slice: x: 4 (x_hi: 2, x_lo: 2; x = x_hi * 2 + x_lo), y: 4, z: 4, core: 2. Of those that a mesh axis runs over, the one named last changes fastest.
Arguments:
- events: bfloat16 [65536, 1024], P(('dp', 'ctx')), parts along dimension 0, may hold values from -48 to 48
- destination: int32 [65536], P(('dp', 'ctx')), parts along dimension 0, may hold values from 0 to 8191, as said below
- segment: int32 [65536], P(('dp', 'ctx')), parts along dimension 0, may hold values from 0 to 3, never falling along the last dimension, each value on 1 to 6144 neighbouring positions
- w_query: bfloat16 [1024, 1024], replicated, may hold values from -0.375 to 0.375
- key_weight: bfloat16 [1024, 256], replicated, may hold values from -0.1875 to 0.1875
- value_weight: bfloat16 [1024, 256], replicated, may hold values from -0.75 to 0.75
Outputs:
- attended: bfloat16 [65536, 1024], P(('dp', 'ctx')), parts along dimension 0
There are 8 independent parts, one for each index of `dp`. A program takes and returns all parts, laid end to end along the dimension named above; an argument that names none is the same for every part. Nothing has to cross between parts.
Inputs may be any that keep to these rules, and one draw needn't show every extreme that they name: destination is a permutation that moves stored events in aligned blocks of 64 rows, keeping their order inside a block; the 8 blocks of one device land on 8 different devices' ranges of 512 packed positions, so at most 64 rows of one device reach one device's range.
All inputs are finite; a program needn't handle non-finite values.
Results may differ from a plain program's by a relative error of at most 0.0045.
The roundings to bfloat16 on the way count: a program that leaves them out, or rounds other values in their place, can miss the bound.
Values may be sent and summed in bfloat16 or wider, within the bound.
No kernel may reach another device: no remote copies, remote signals or barrier semaphores. Data moves between devices by JAX's collectives and lax.ppermute only.
A program may use at most 64 MiB of HBM per device.

v0:
```python
import math

import jax
import jax.numpy as jnp
from jax import lax
from jax.sharding import PartitionSpec as P

QUERY_HEADS = 8
KEY_VALUE_HEADS = 2
HEAD_SIZE = 128
BLOCKS = 8


NEGATIVE_FILL = -1e30


def on_device(events, destination, segment, w_query, key_weight, value_weight):
    token_count = events.shape[0]
    width = events.shape[1]
    ndevices = lax.axis_size("ctx")
    myself = lax.axis_index("ctx")
    group_size = QUERY_HEADS // KEY_VALUE_HEADS
    score_scale = 1.0 / math.sqrt(HEAD_SIZE)
    lanes = jnp.arange(ndevices, dtype=jnp.int32)
    local_rows = jnp.arange(token_count, dtype=jnp.int32)
    target = destination // token_count
    place = destination % token_count
    bucket = token_count // BLOCKS
    own_position = myself * token_count + local_rows
    onehot = (target[:, None] == lanes[None, :]).astype(jnp.int32)
    before = jnp.cumsum(onehot, axis=0) - onehot
    slot = jnp.sum(before * onehot, axis=1)
    index = target * bucket + slot
    send_rows = (
        jnp.zeros((ndevices * bucket, width), events.dtype)
        .at[index]
        .set(events)
        .reshape(ndevices, bucket, width)
    )
    send_place = (
        jnp.full((ndevices * bucket,), token_count, jnp.int32)
        .at[index]
        .set(place)
        .reshape(ndevices, bucket)
    )
    got_rows, got_place = (
        lax.all_to_all(send_rows, "ctx", split_axis=0, concat_axis=0, tiled=True),
        lax.all_to_all(send_place, "ctx", split_axis=0, concat_axis=0, tiled=True),
    )
    packed = (
        jnp.zeros((token_count, width), events.dtype)
        .at[got_place.reshape(-1)]
        .set(got_rows.reshape(-1, width), mode="drop")
    )
    query_rows = jnp.dot(packed, w_query, preferred_element_type=jnp.float32).astype(jnp.bfloat16)
    key_rows = jnp.dot(packed, key_weight, preferred_element_type=jnp.float32).astype(jnp.bfloat16)
    value_rows = jnp.dot(packed, value_weight, preferred_element_type=jnp.float32).astype(
        jnp.bfloat16
    )
    query_head_rows = query_rows.reshape(token_count, KEY_VALUE_HEADS, group_size, HEAD_SIZE)
    query_seg = segment.astype(jnp.float32)
    seg_sent = segment.astype(jnp.bfloat16)
    start_state = (
        jnp.full((KEY_VALUE_HEADS, group_size, token_count), NEGATIVE_FILL, jnp.float32),
        jnp.zeros((KEY_VALUE_HEADS, group_size, token_count), jnp.float32),
        jnp.zeros((KEY_VALUE_HEADS, group_size, token_count, HEAD_SIZE), jnp.float32),
    )
    carry = start_state
    key_portion = lax.all_gather(key_rows, "ctx", axis=0, tiled=True)
    value_portion = lax.all_gather(value_rows, "ctx", axis=0, tiled=True)
    seg_piece = lax.all_gather(seg_sent, "ctx", axis=0, tiled=True)
    token_rows = key_portion.shape[0]
    block_step = 512
    event_count = token_rows // block_step
    key_block_list = key_portion.reshape(event_count, block_step, KEY_VALUE_HEADS, HEAD_SIZE)
    value_block_list = value_portion.reshape(event_count, block_step, KEY_VALUE_HEADS, HEAD_SIZE)
    seg_blocks = seg_piece.astype(jnp.float32).reshape(event_count, block_step)
    offsets = jnp.arange(event_count, dtype=jnp.int32) * block_step

    def one_block(state, inputs):
        key_tile_rows, value_block, seg_block, offset = inputs
        key_pos = offset + jnp.arange(block_step, dtype=jnp.int32)
        allowed = (seg_block[None, :] == query_seg[:, None]) & (
            key_pos[None, :] <= own_position[:, None]
        )
        best, total_tokens, accum = state
        logit_scores = (
            jnp.einsum(
                "qxli,oxi->xlqo", query_head_rows, key_tile_rows, preferred_element_type=jnp.float32
            )
            * score_scale
        )
        logit_scores = jnp.where(allowed, logit_scores, NEGATIVE_FILL)
        fresh = jnp.maximum(best, jnp.max(logit_scores, axis=-1))
        softmax_weights = jnp.where(allowed, jnp.exp(logit_scores - fresh[..., None]), 0.0)
        shrink = jnp.exp(best - fresh)
        total_tokens = total_tokens * shrink + jnp.sum(softmax_weights, axis=-1)
        accum = accum * shrink[..., None] + jnp.einsum(
            "qlwc,cqh->qlwh",
            softmax_weights.astype(jnp.bfloat16),
            value_block,
            preferred_element_type=jnp.float32,
        )
        state = (fresh, total_tokens, accum)
        return (state, None)

    carry, _ = lax.scan(one_block, carry, (key_block_list, value_block_list, seg_blocks, offsets))
    best, total_tokens, accum = carry
    result = (
        (accum / total_tokens[..., None])
        .transpose(2, 0, 1, 3)
        .reshape(token_count, QUERY_HEADS * HEAD_SIZE)
        .astype(jnp.bfloat16)
    )
    return result


def solution(mesh):
    return jax.shard_map(
        on_device,
        mesh=mesh,
        in_specs=(P(("dp", "ctx"), None), P(("dp", "ctx")), P(("dp", "ctx")), P(), P(), P()),
        out_specs=P(("dp", "ctx"), None),
        check_vma=False,
    )
```

profile of v0, /device:TPU:1, one launch (start us, length us, event | category | flops | bytes accessed | tf_op | source)
XLA Modules:
  0.0 347.3 jit_solution(6097771895671642066)
XLA Ops:
  8.9 2.4 scatter_custom_fusion
  12.0 6.9 %all-to-all-start = ((s32[16,1,64]{2,1,0:T(1,128)}), s32[16,1,64]{2,1,0:T(1,128)S(1)}, u32[]{:S(2)}, u32[]{:S(2)}) async-start(s32[16,1,64]{2,1,0:T(1,128)} %all_to_all.9), calls=%async_computation | async-start | bytes 16384 | tf_op jit(solution)/shard_map/all_to_all | solution.py:48
  18.9 4.8 %scatter_custom_fusion.1 = bf16[1024,1024]{1,0:T(8,128)(2,1)} fusion(s32[512]{0:T(512)S(1)} %compare_select_fusion.1, bf16[512,1024]{1,0:T(8,128)(2,1)} %param.8, bf16[]{:T(256)} %constant.62.clone.1), kind=kCustom, calls=%fused_computation.33 | custom fusion | bytes 2097664 | tf_op jit(solution)/shard_map/scatter | solution.py:37
  24.4 5.2 %all-to-all-start.1 = ((bf16[16,64,1024]{2,1,0:T(8,128)(2,1)}), bf16[16,64,1024]{2,1,0:T(8,128)(2,1)}, u32[]{:S(2)}, u32[]{:S(2)}) async-start(bf16[16,64,1024]{2,1,0:T(8,128)(2,1)} %bitcast.83), calls=%async_computation.1 | async-start | bytes 4194304 | tf_op jit(solution)/shard_map/all_to_all | solution.py:47
  30.9 26.4 %all-to-all-done.1 = bf16[16,64,1024]{2,1,0:T(8,128)(2,1)} async-done(((bf16[16,64,1024]{2,1,0:T(8,128)(2,1)}), bf16[16,64,1024]{2,1,0:T(8,128)(2,1)}, u32[]{:S(2)}, u32[]{:S(2)}) %all-to-all-start.1) | async-done | bytes 2097184 | tf_op jit(solution)/shard_map/all_to_all | solution.py:47
  57.3 6.2 %scatter_custom_fusion.2 = bf16[512,1024]{1,0:T(8,128)(2,1)S(1)} fusion(s32[1024]{0:T(1024)S(1)} %bitcast.87, bf16[1024,1024]{1,0:T(8,128)(2,1)} %bitcast.4, bf16[]{:T(256)} %constant.62.clone.1), kind=kCustom, calls=%fused_computation.36 | custom fusion | bytes 1049088 | tf_op jit(solution)/shard_map/scatter | solution.py:53
  63.4 2.2 convolution_convert_fusion.1
  65.7 2.2 convolution_convert_fusion.2
  68.0 21.0 %all-gather = bf16[16,1,512]{2,1,0:T(2,128)(2,1)S(1)} all-gather(bf16[1,1,512]{2,1,0:T(2,128)(2,1)S(1)} %reshape.121), channel_id=1, replica_groups=mesh['dp'=8,'ctx'=16] {'ctx'}, dimensions={0}, use_global_device_ids=true | all-gather | bytes 17408 | tf_op jit(solution)/shard_map/all_gather | solution.py:71
  89.0 2.2 convolution_convert_fusion
  91.2 2.6 reshape.91
  95.2 11.1 %all-gather.6.cloned.1.call-done = bf16[8192,256]{1,0:T(8,128)(2,1)} async-done(((bf16[512,256]{1,0:T(8,128)(2,1)}), bf16[8192,256]{1,0:T(8,128)(2,1)}) %all-gather.6.cloned.1.call-update) | async-done | bytes 4194320 | tf_op jit(solution)/shard_map/all_gather | solution.py:70
  106.3 6.9 %reshape.92 = bf16[16,512,2,128]{3,2,1,0:T(2,128)(2,1)} reshape(bf16[8192,256]{1,0:T(8,128)(2,1)} %all-gather.6.cloned.1.call-done) | data formatting | bytes 8388608 | tf_op jit(solution)/shard_map/reshape | solution.py:76
  113.2 31.8 %all-gather.4.cloned.1.call-done = bf16[8192,256]{1,0:T(8,128)(2,1)} async-done(((bf16[512,256]{1,0:T(8,128)(2,1)}), bf16[8192,256]{1,0:T(8,128)(2,1)}) %all-gather.4.cloned.1.call-update) | async-done | bytes 4194320 | tf_op jit(solution)/shard_map/all_gather | solution.py:69
  145.0 6.9 %reshape.90 = bf16[16,512,2,128]{3,2,1,0:T(2,128)(2,1)} reshape(bf16[8192,256]{1,0:T(8,128)(2,1)} %all-gather.4.cloned.1.call-done) | data formatting | bytes 8388608 | tf_op jit(solution)/shard_map/reshape | solution.py:75
  151.9 184.2 %while.15 = (s32[]{:T(128)}, f32[2,4,512]{2,1,0:T(4,128)S(1)}, f32[2,4,512]{2,1,0:T(4,128)S(1)}, f32[2,4,512,128]{3,2,1,0:T(8,128)}, f32[16,512]{1,0:T(8,128)S(1...) while((s32[]{:T(128)}, f32[2,4,512]{2,1,0:T(4,128)S(1)}, ...), condition=%wide.region_9.10_spmd.clone, body=%wide.region_6.9_spmd.clone.sunk | while | flops 1103385600 | bytes 50086116 | solution.py:107
  158.5 3.5 %fusion.47 = f32[2,4,512,128]{3,2,1,0:T(8,128)S(1)} fusion(f32[2,4,512,128]{3,2,1,0:T(8,128)S(1)} %copy-done.1, f32[2,512,512,4]{2,1,3,0:T(8,128)S(1)} %get-tuple-element.250, f32[2,4,512]{2,1,0:T(4,128)S(1)} %select_maximum_fusion.2, pred[512,512]{0,1:T(8,128)(4,1)S(1)} %compare_and_fusion.2, f32[2,4,512]{2,1,0:T(4,128)S(1)} %get-tuple-element.252, ...), kind=kOutput, calls=%fused_computation.12.clone.1 | convolution fusion | flops 548929536 | bytes 13139969 | tf_op jit(solution)/shard_map/while/body/eval_jaxpr/qlwc,cqh->qlwh/dot_general | solution.py:98
  170.1 3.5 %fusion.47 = f32[2,4,512,128]{3,2,1,0:T(8,128)S(1)} fusion(f32[2,4,512,128]{3,2,1,0:T(8,128)S(1)} %copy-done.1, f32[2,512,512,4]{2,1,3,0:T(8,128)S(1)} %get-tuple-element.250, f32[2,4,512]{2,1,0:T(4,128)S(1)} %select_maximum_fusion.2, pred[512,512]{0,1:T(8,128)(4,1)S(1)} %compare_and_fusion.2, f32[2,4,512]{2,1,0:T(4,128)S(1)} %get-tuple-element.252, ...), kind=kOutput, calls=%fused_computation.12.clone.1 | convolution fusion | flops 548929536 | bytes 13139969 | tf_op jit(solution)/shard_map/while/body/eval_jaxpr/qlwc,cqh->qlwh/dot_general | solution.py:98
  181.6 3.5 %fusion.47 = f32[2,4,512,128]{3,2,1,0:T(8,128)S(1)} fusion(f32[2,4,512,128]{3,2,1,0:T(8,128)S(1)} %copy-done.1, f32[2,512,512,4]{2,1,3,0:T(8,128)S(1)} %get-tuple-element.250, f32[2,4,512]{2,1,0:T(4,128)S(1)} %select_maximum_fusion.2, pred[512,512]{0,1:T(8,128)(4,1)S(1)} %compare_and_fusion.2, f32[2,4,512]{2,1,0:T(4,128)S(1)} %get-tuple-element.252, ...), kind=kOutput, calls=%fused_computation.12.clone.1 | convolution fusion | flops 548929536 | bytes 13139969 | tf_op jit(solution)/shard_map/while/body/eval_jaxpr/qlwc,cqh->qlwh/dot_general | solution.py:98
  193.1 3.5 %fusion.47 = f32[2,4,512,128]{3,2,1,0:T(8,128)S(1)} fusion(f32[2,4,512,128]{3,2,1,0:T(8,128)S(1)} %copy-done.1, f32[2,512,512,4]{2,1,3,0:T(8,128)S(1)} %get-tuple-element.250, f32[2,4,512]{2,1,0:T(4,128)S(1)} %select_maximum_fusion.2, pred[512,512]{0,1:T(8,128)(4,1)S(1)} %compare_and_fusion.2, f32[2,4,512]{2,1,0:T(4,128)S(1)} %get-tuple-element.252, ...), kind=kOutput, calls=%fused_computation.12.clone.1 | convolution fusion | flops 548929536 | bytes 13139969 | tf_op jit(solution)/shard_map/while/body/eval_jaxpr/qlwc,cqh->qlwh/dot_general | solution.py:98
  204.6 3.5 %fusion.47 = f32[2,4,512,128]{3,2,1,0:T(8,128)S(1)} fusion(f32[2,4,512,128]{3,2,1,0:T(8,128)S(1)} %copy-done.1, f32[2,512,512,4]{2,1,3,0:T(8,128)S(1)} %get-tuple-element.250, f32[2,4,512]{2,1,0:T(4,128)S(1)} %select_maximum_fusion.2, pred[512,512]{0,1:T(8,128)(4,1)S(1)} %compare_and_fusion.2, f32[2,4,512]{2,1,0:T(4,128)S(1)} %get-tuple-element.252, ...), kind=kOutput, calls=%fused_computation.12.clone.1 | convolution fusion | flops 548929536 | bytes 13139969 | tf_op jit(solution)/shard_map/while/body/eval_jaxpr/qlwc,cqh->qlwh/dot_general | solution.py:98
  216.1 3.5 %fusion.47 = f32[2,4,512,128]{3,2,1,0:T(8,128)S(1)} fusion(f32[2,4,512,128]{3,2,1,0:T(8,128)S(1)} %copy-done.1, f32[2,512,512,4]{2,1,3,0:T(8,128)S(1)} %get-tuple-element.250, f32[2,4,512]{2,1,0:T(4,128)S(1)} %select_maximum_fusion.2, pred[512,512]{0,1:T(8,128)(4,1)S(1)} %compare_and_fusion.2, f32[2,4,512]{2,1,0:T(4,128)S(1)} %get-tuple-element.252, ...), kind=kOutput, calls=%fused_computation.12.clone.1 | convolution fusion | flops 548929536 | bytes 13139969 | tf_op jit(solution)/shard_map/while/body/eval_jaxpr/qlwc,cqh->qlwh/dot_general | solution.py:98
  227.6 3.5 %fusion.47 = f32[2,4,512,128]{3,2,1,0:T(8,128)S(1)} fusion(f32[2,4,512,128]{3,2,1,0:T(8,128)S(1)} %copy-done.1, f32[2,512,512,4]{2,1,3,0:T(8,128)S(1)} %get-tuple-element.250, f32[2,4,512]{2,1,0:T(4,128)S(1)} %select_maximum_fusion.2, pred[512,512]{0,1:T(8,128)(4,1)S(1)} %compare_and_fusion.2, f32[2,4,512]{2,1,0:T(4,128)S(1)} %get-tuple-element.252, ...), kind=kOutput, calls=%fused_computation.12.clone.1 | convolution fusion | flops 548929536 | bytes 13139969 | tf_op jit(solution)/shard_map/while/body/eval_jaxpr/qlwc,cqh->qlwh/dot_general | solution.py:98
  239.2 3.5 %fusion.47 = f32[2,4,512,128]{3,2,1,0:T(8,128)S(1)} fusion(f32[2,4,512,128]{3,2,1,0:T(8,128)S(1)} %copy-done.1, f32[2,512,512,4]{2,1,3,0:T(8,128)S(1)} %get-tuple-element.250, f32[2,4,512]{2,1,0:T(4,128)S(1)} %select_maximum_fusion.2, pred[512,512]{0,1:T(8,128)(4,1)S(1)} %compare_and_fusion.2, f32[2,4,512]{2,1,0:T(4,128)S(1)} %get-tuple-element.252, ...), kind=kOutput, calls=%fused_computation.12.clone.1 | convolution fusion | flops 548929536 | bytes 13139969 | tf_op jit(solution)/shard_map/while/body/eval_jaxpr/qlwc,cqh->qlwh/dot_general | solution.py:98
  250.7 3.5 %fusion.47 = f32[2,4,512,128]{3,2,1,0:T(8,128)S(1)} fusion(f32[2,4,512,128]{3,2,1,0:T(8,128)S(1)} %copy-done.1, f32[2,512,512,4]{2,1,3,0:T(8,128)S(1)} %get-tuple-element.250, f32[2,4,512]{2,1,0:T(4,128)S(1)} %select_maximum_fusion.2, pred[512,512]{0,1:T(8,128)(4,1)S(1)} %compare_and_fusion.2, f32[2,4,512]{2,1,0:T(4,128)S(1)} %get-tuple-element.252, ...), kind=kOutput, calls=%fused_computation.12.clone.1 | convolution fusion | flops 548929536 | bytes 13139969 | tf_op jit(solution)/shard_map/while/body/eval_jaxpr/qlwc,cqh->qlwh/dot_general | solution.py:98
  262.2 3.5 %fusion.47 = f32[2,4,512,128]{3,2,1,0:T(8,128)S(1)} fusion(f32[2,4,512,128]{3,2,1,0:T(8,128)S(1)} %copy-done.1, f32[2,512,512,4]{2,1,3,0:T(8,128)S(1)} %get-tuple-element.250, f32[2,4,512]{2,1,0:T(4,128)S(1)} %select_maximum_fusion.2, pred[512,512]{0,1:T(8,128)(4,1)S(1)} %compare_and_fusion.2, f32[2,4,512]{2,1,0:T(4,128)S(1)} %get-tuple-element.252, ...), kind=kOutput, calls=%fused_computation.12.clone.1 | convolution fusion | flops 548929536 | bytes 13139969 | tf_op jit(solution)/shard_map/while/body/eval_jaxpr/qlwc,cqh->qlwh/dot_general | solution.py:98
  273.7 3.5 %fusion.47 = f32[2,4,512,128]{3,2,1,0:T(8,128)S(1)} fusion(f32[2,4,512,128]{3,2,1,0:T(8,128)S(1)} %copy-done.1, f32[2,512,512,4]{2,1,3,0:T(8,128)S(1)} %get-tuple-element.250, f32[2,4,512]{2,1,0:T(4,128)S(1)} %select_maximum_fusion.2, pred[512,512]{0,1:T(8,128)(4,1)S(1)} %compare_and_fusion.2, f32[2,4,512]{2,1,0:T(4,128)S(1)} %get-tuple-element.252, ...), kind=kOutput, calls=%fused_computation.12.clone.1 | convolution fusion | flops 548929536 | bytes 13139969 | tf_op jit(solution)/shard_map/while/body/eval_jaxpr/qlwc,cqh->qlwh/dot_general | solution.py:98
  285.2 3.5 %fusion.47 = f32[2,4,512,128]{3,2,1,0:T(8,128)S(1)} fusion(f32[2,4,512,128]{3,2,1,0:T(8,128)S(1)} %copy-done.1, f32[2,512,512,4]{2,1,3,0:T(8,128)S(1)} %get-tuple-element.250, f32[2,4,512]{2,1,0:T(4,128)S(1)} %select_maximum_fusion.2, pred[512,512]{0,1:T(8,128)(4,1)S(1)} %compare_and_fusion.2, f32[2,4,512]{2,1,0:T(4,128)S(1)} %get-tuple-element.252, ...), kind=kOutput, calls=%fused_computation.12.clone.1 | convolution fusion | flops 548929536 | bytes 13139969 | tf_op jit(solution)/shard_map/while/body/eval_jaxpr/qlwc,cqh->qlwh/dot_general | solution.py:98
  296.7 3.5 %fusion.47 = f32[2,4,512,128]{3,2,1,0:T(8,128)S(1)} fusion(f32[2,4,512,128]{3,2,1,0:T(8,128)S(1)} %copy-done.1, f32[2,512,512,4]{2,1,3,0:T(8,128)S(1)} %get-tuple-element.250, f32[2,4,512]{2,1,0:T(4,128)S(1)} %select_maximum_fusion.2, pred[512,512]{0,1:T(8,128)(4,1)S(1)} %compare_and_fusion.2, f32[2,4,512]{2,1,0:T(4,128)S(1)} %get-tuple-element.252, ...), kind=kOutput, calls=%fused_computation.12.clone.1 | convolution fusion | flops 548929536 | bytes 13139969 | tf_op jit(solution)/shard_map/while/body/eval_jaxpr/qlwc,cqh->qlwh/dot_general | solution.py:98
  308.3 3.5 %fusion.47 = f32[2,4,512,128]{3,2,1,0:T(8,128)S(1)} fusion(f32[2,4,512,128]{3,2,1,0:T(8,128)S(1)} %copy-done.1, f32[2,512,512,4]{2,1,3,0:T(8,128)S(1)} %get-tuple-element.250, f32[2,4,512]{2,1,0:T(4,128)S(1)} %select_maximum_fusion.2, pred[512,512]{0,1:T(8,128)(4,1)S(1)} %compare_and_fusion.2, f32[2,4,512]{2,1,0:T(4,128)S(1)} %get-tuple-element.252, ...), kind=kOutput, calls=%fused_computation.12.clone.1 | convolution fusion | flops 548929536 | bytes 13139969 | tf_op jit(solution)/shard_map/while/body/eval_jaxpr/qlwc,cqh->qlwh/dot_general | solution.py:98
  319.8 3.5 %fusion.47 = f32[2,4,512,128]{3,2,1,0:T(8,128)S(1)} fusion(f32[2,4,512,128]{3,2,1,0:T(8,128)S(1)} %copy-done.1, f32[2,512,512,4]{2,1,3,0:T(8,128)S(1)} %get-tuple-element.250, f32[2,4,512]{2,1,0:T(4,128)S(1)} %select_maximum_fusion.2, pred[512,512]{0,1:T(8,128)(4,1)S(1)} %compare_and_fusion.2, f32[2,4,512]{2,1,0:T(4,128)S(1)} %get-tuple-element.252, ...), kind=kOutput, calls=%fused_computation.12.clone.1 | convolution fusion | flops 548929536 | bytes 13139969 | tf_op jit(solution)/shard_map/while/body/eval_jaxpr/qlwc,cqh->qlwh/dot_general | solution.py:98
  331.3 3.5 %fusion.47 = f32[2,4,512,128]{3,2,1,0:T(8,128)S(1)} fusion(f32[2,4,512,128]{3,2,1,0:T(8,128)S(1)} %copy-done.1, f32[2,512,512,4]{2,1,3,0:T(8,128)S(1)} %get-tuple-element.250, f32[2,4,512]{2,1,0:T(4,128)S(1)} %select_maximum_fusion.2, pred[512,512]{0,1:T(8,128)(4,1)S(1)} %compare_and_fusion.2, f32[2,4,512]{2,1,0:T(4,128)S(1)} %get-tuple-element.252, ...), kind=kOutput, calls=%fused_computation.12.clone.1 | convolution fusion | flops 548929536 | bytes 13139969 | tf_op jit(solution)/shard_map/while/body/eval_jaxpr/qlwc,cqh->qlwh/dot_general | solution.py:98
  (257 shorter events, 137.6 us)
Async XLA Ops:
  6.5 82.5 %copy-start = (bf16[1024,1024]{1,0:T(8,128)(2,1)S(1)}, bf16[1024,1024]{1,0:T(8,128)(2,1)}, u32[]{:S(2)}) copy-start(bf16[1024,1024]{1,0:T(8,128)(2,1)} %param.11) | copy-start | bytes 6291460
  12.0 12.3 %all-to-all-start = ((s32[16,1,64]{2,1,0:T(1,128)}), s32[16,1,64]{2,1,0:T(1,128)S(1)}, u32[]{:S(2)}, u32[]{:S(2)}) async-start(s32[16,1,64]{2,1,0:T(1,128)} %all_to_all.9), calls=%async_computation | async-start | bytes 16384 | tf_op jit(solution)/shard_map/all_to_all | solution.py:48
  24.4 43.6 %copy-start.3 = (s32[512]{0:T(512)S(1)}, s32[512]{0:T(512)}, u32[]{:S(2)}) copy-start(s32[512]{0:T(512)} %param.10) | copy-start | bytes 6148
  24.4 32.9 %all-to-all-start.1 = ((bf16[16,64,1024]{2,1,0:T(8,128)(2,1)}), bf16[16,64,1024]{2,1,0:T(8,128)(2,1)}, u32[]{:S(2)}, u32[]{:S(2)}) async-start(bf16[16,64,1024]{2,1,0:T(8,128)(2,1)} %bitcast.83), calls=%async_computation.1 | async-start | bytes 4194304 | tf_op jit(solution)/shard_map/all_to_all | solution.py:47
  29.6 76.7 %all-gather.6.cloned.1.call-start = ((), (), s32[]{:S(2)}) async-start(), calls=%async_computation.3 | async-start | bytes 4456448 | tf_op jit(solution)/shard_map/all_gather | solution.py:70
  65.7 79.3 %all-gather.4.cloned.1.call-start = ((), (), s32[]{:S(2)}) async-start(), calls=%async_computation.2 | async-start | bytes 4456448 | tf_op jit(solution)/shard_map/all_gather | solution.py:69
  156.4 2.1 copy-start.1
  162.1 1.4 copy-start.2
  168.0 2.1 copy-start.1
  173.6 1.4 copy-start.2
  179.5 2.1 copy-start.1
  185.1 1.4 copy-start.2
  191.0 2.1 copy-start.1
  196.6 1.4 copy-start.2
  202.5 2.1 copy-start.1
  208.1 1.4 copy-start.2
  214.0 2.1 copy-start.1
  219.6 1.4 copy-start.2
  225.5 2.1 copy-start.1
  231.2 1.4 copy-start.2
  237.1 2.1 copy-start.1
  242.7 1.4 copy-start.2
  248.6 2.1 copy-start.1
  254.2 1.4 copy-start.2
  260.1 2.1 copy-start.1
  265.7 1.4 copy-start.2
  271.6 2.1 copy-start.1
  283.1 2.1 copy-start.1
  294.6 2.1 copy-start.1
  306.1 2.1 copy-start.1
  317.7 2.1 copy-start.1
  329.2 2.1 copy-start.1
  (6 other events, 8.2 us)
Sparse Core Ops, SparseCore 0:
  65.8 40.4 all-gather.5
  108.0 36.9 all-gather.3
where the time goes:
time: 349 us; the launch traced here: 347 us
  local copies, waits for them, and re-layouts  88.4 us (25%)
  matrix products  88.2 us (25%)
  waiting for transfers between devices  70 us (20%)
  other arithmetic  52.9 us (15%)
  blocking collectives  21 us (6%)
  between operations  13.5 us (4%)
  starting transfers between devices  12.2 us (3%)
    dot_general x16, matrix products, one_block(): jnp.einsum('qlwc,cqh->qlwh', softmax_weights.astype(jnp.bfloat16), value_...  56.2 us
    reduce_sum x16, other arithmetic, one_block(): total_tokens = total_tokens * shrink + jnp.sum(softmax_weights, axis=-1)  32.7 us
    all_gather x1, waiting for transfers between devices, on_device(): key_portion = lax.all_gather(key_rows, 'ctx', axis=0, tiled=True)  31.8 us
    dynamic_slice x48, local copies, waits for them, and re-layouts, on_device(): lax.scan(one_block, carry, (key_block_list, value_block_list, seg_blocks,...  31.8 us
    all_to_all x1, waiting for transfers between devices, on_device(): lax.all_to_all(send_rows, 'ctx', split_axis=0, concat_axis=0, tiled=True)  26.4 us
    dot_general x16, matrix products, one_block(): jnp.einsum('qxli,oxi->xlqo', query_head_rows, key_tile_rows, preferred_el...  25.3 us
    while x80, local copies, waits for them, and re-layouts  21.6 us
    all_gather x1, blocking collectives, on_device(): seg_piece = lax.all_gather(seg_sent, 'ctx', axis=0, tiled=True)  21 us
  transfers between devices with their start and end apart: 4, of which 4 were waited for; matrix products, arithmetic and copies ran while one was open for 6% of the time, Pallas kernels for 0%

commit v1 on v0

v1 whole, which is shorter than its diff:
```python
import math

import jax
import jax.numpy as jnp
from jax import lax
from jax.experimental import pallas as pl
from jax.experimental.pallas import tpu as pltpu
from jax.sharding import PartitionSpec as P


QUERY_HEADS = 8
KEY_VALUE_HEADS = 2
HEAD_SIZE = 128
GROUP = QUERY_HEADS // KEY_VALUE_HEADS
BLK = 64
META = 16
NEGATIVE_FILL = -1e30
SCALE2 = math.log2(math.e) / math.sqrt(HEAD_SIZE)
TK = 1024
TQ = 512


VMEM = pltpu.VMEM
SMEM = pltpu.SMEM


def lower_bound(ref, value, size):
    low = jnp.int32(0)
    step = size
    while step >= 1:
        probe = low + step
        inside = probe <= size
        entry = ref[jnp.minimum(probe, size) - 1]
        low = jnp.where(inside & (entry < value), probe, low)
        step //= 2
    return low


def kv_kernel(core_ref, dest_ref, seg_ref, ev_ref, kw_ref, vw_ref, own_ref, send_ref):
    rows = ev_ref.shape[0]
    core = core_ref[0]
    events = ev_ref[...]
    keys = jnp.dot(events, kw_ref[...], preferred_element_type=jnp.float32).astype(jnp.bfloat16)
    values = jnp.dot(events, vw_ref[...], preferred_element_type=jnp.float32).astype(jnp.bfloat16)

    def put(ref, head):
        cols = slice(head * HEAD_SIZE, (head + 1) * HEAD_SIZE)
        ref[:rows, :HEAD_SIZE] = keys[:, cols]
        ref[:rows, HEAD_SIZE:] = values[:, cols]

    @pl.when(core == 0)
    def _():
        put(own_ref, 0)
        put(send_ref, 1)

    @pl.when(core != 0)
    def _():
        put(own_ref, 1)
        put(send_ref, 0)

    lane = lax.broadcasted_iota(jnp.int32, (META, 2 * HEAD_SIZE), 1)
    meta = jnp.zeros((META, 2 * HEAD_SIZE), jnp.int32)
    for b in range(rows // BLK):
        meta = jnp.where(lane == b, dest_ref[b * BLK] // BLK, meta)
    for s in range(3):
        below = lower_bound(seg_ref, s + 1, rows)
        first = jnp.minimum(below, rows // 2)
        meta = jnp.where(lane == 16 + 2 * s, first, meta)
        meta = jnp.where(lane == 17 + 2 * s, below - first, meta)
    packed = meta.astype(jnp.float32).astype(jnp.bfloat16)
    own_ref[rows : rows + META, :] = packed
    send_ref[rows:, :] = packed


def q_kernel(dest_ref, ev_ref, wq_ref, after_ref, out_ref, q_ref, sem):
    del after_ref
    rows = ev_ref.shape[0]
    half = GROUP * HEAD_SIZE
    for g in range(KEY_VALUE_HEADS):
        q_ref[g] = jnp.dot(
            ev_ref[...], wq_ref[:, g * half : (g + 1) * half], preferred_element_type=jnp.float32
        ).astype(jnp.bfloat16)
    copies = []
    for b in range(rows // BLK):
        target = dest_ref[b * BLK] // rows
        chip = target // 2
        side = target % 2
        for g in range(KEY_VALUE_HEADS):
            copies.append(
                pltpu.make_async_copy(
                    q_ref.at[g, pl.ds(b * BLK, BLK), :],
                    out_ref.at[chip * 2 + g, side],
                    sem.at[b * KEY_VALUE_HEADS + g],
                )
            )
            copies[-1].start()
    for copy in copies:
        copy.wait()


def attention_kernel(where_ref, *refs):
    shards = refs[:8]
    q_in_ref, own_out, send_out = refs[8:11]
    kv, v_t, q_buf, q_t, meta_bf, meta_int, table, m_ref, l_ref, acc_ref, sem, meta_sem = refs[11:]
    chip_x, chip_y, core = where_ref[0], where_ref[1], where_ref[2]
    per_dev = (kv.shape[0] - TK) // 16
    shard_rows = per_dev + META
    blocks = per_dev // BLK
    offsets = [(0, 0), (0, 3), (0, 1), (1, 0), (1, 3), (0, 2), (1, 1), (1, 2)]

    def source(i, h):
        return shards[i], h * shard_rows

    fetches = []
    for i in range(8):
        for h in range(2):
            ref, base = source(i, h)
            copy = pltpu.make_async_copy(
                ref.at[pl.ds(base + per_dev, META), :], meta_bf.at[i * 2 + h], meta_sem.at[i * 2 + h]
            )
            copy.start()
            fetches.append(copy)
    for copy in fetches:
        copy.wait()
    meta = meta_bf[:, 0, :HEAD_SIZE].astype(jnp.float32).astype(jnp.int32)
    lane = lax.broadcasted_iota(jnp.int32, meta.shape, 1)
    total = jnp.sum(meta, axis=0, keepdims=True)
    meta_int[...] = jnp.where(lane < 16, meta, jnp.broadcast_to(total, meta.shape))
    copy = pltpu.make_async_copy(meta_int, table, meta_sem.at[0])
    copy.start()
    copy.wait()

    my_chip = chip_x * 4 + chip_y
    for i, (dx, dy) in enumerate(offsets):
        chip = (chip_x + dx) % 2 * 4 + (chip_y + dy) % 4
        for h in range(2):
            ref, base = source(i, h)
            device = chip * 2 + (core if h == 0 else 1 - core)

            def place(b, carry, ref=ref, base=base, device=device, i=i, h=h):
                j = table[i * 2 + h, b]
                pltpu.make_async_copy(
                    ref.at[pl.ds(base + b * BLK, BLK), :], kv.at[pl.ds(j * BLK, BLK), :], sem.at[0]
                ).start()

                @pl.when(j // (2 * blocks) == my_chip)
                def _():
                    local = j - my_chip * 2 * blocks
                    pltpu.make_async_copy(
                        q_in_ref.at[device, local // blocks], q_buf.at[pl.ds(local * BLK, BLK), :], sem.at[1]
                    ).start()

                return carry

            lax.fori_loop(0, blocks, place, 0)
    bound = [table[0, 16 + 2 * s] + table[0, 17 + 2 * s] for s in range(3)]

    def start_of(pos):
        begin = jnp.zeros_like(pos)
        for b in bound:
            begin = jnp.where(pos >= b, jnp.maximum(begin, b), begin)
        return begin

    rows_all = pl.ds(0, 16 * per_dev)
    kv[16 * per_dev :, :] = jnp.zeros((TK, 2 * HEAD_SIZE), jnp.bfloat16)
    pltpu.make_async_copy(kv.at[rows_all], kv.at[rows_all], sem.at[0]).wait()
    pltpu.make_async_copy(q_buf, q_buf, sem.at[1]).wait()

    chip_rows = 2 * per_dev
    first = my_chip * chip_rows
    anchor = start_of(first) // BLK * BLK

    def turn(t, carry):
        rows = pl.ds(pl.multiple_of(anchor + t * TK, BLK), TK)
        v_t[t] = kv[rows, HEAD_SIZE:].T
        return carry

    lax.fori_loop(0, (first + chip_rows - anchor + TK - 1) // TK, turn, 0)

    for tq in range(chip_rows // TQ):
        p0 = first + tq * TQ
        low_first = start_of(p0)
        low_last = start_of(p0 + TQ - 1)
        for h in range(GROUP):
            q = q_buf[tq * TQ : (tq + 1) * TQ, h * HEAD_SIZE : (h + 1) * HEAD_SIZE]
            q = q.astype(jnp.float32) * SCALE2
            high = q.astype(jnp.bfloat16)
            q_t[h, :HEAD_SIZE] = high.T
            q_t[h, HEAD_SIZE:] = (q - high.astype(jnp.float32)).astype(jnp.bfloat16).T
            m_ref[h] = jnp.full((1, TQ), NEGATIVE_FILL, jnp.float32)
            l_ref[h] = jnp.zeros((1, TQ), jnp.float32)
            acc_ref[h] = jnp.zeros((HEAD_SIZE, TQ), jnp.float32)

        def tile(t, masked, p0=p0):
            k0 = pl.multiple_of(anchor + t * TK, BLK)
            k = kv[pl.ds(k0, TK), :HEAD_SIZE]
            k = jnp.concatenate([k, k], axis=1)
            v = v_t[t]
            if masked:
                kpos = k0 + lax.broadcasted_iota(jnp.int32, (TK, TQ), 0)
                qpos = p0 + lax.broadcasted_iota(jnp.int32, (1, TQ), 1)
                allowed = (kpos <= qpos) & (kpos >= start_of(qpos))

            def score(h):
                s = jnp.dot(k, q_t[h], preferred_element_type=jnp.float32)
                return jnp.where(allowed, s, NEGATIVE_FILL) if masked else s

            s = score(0)
            for h in range(GROUP):
                following = score(h + 1) if h + 1 < GROUP else None
                m_old = m_ref[h]
                m_new = jnp.maximum(m_old, jnp.max(s, axis=0, keepdims=True))
                p = jnp.exp2(s - m_new)
                shrink = jnp.exp2(m_old - m_new)
                m_ref[h] = m_new
                l_ref[h] = l_ref[h] * shrink + jnp.sum(p, axis=0, keepdims=True)
                acc_ref[h] = acc_ref[h] * shrink + jnp.dot(
                    v, p.astype(jnp.bfloat16), preferred_element_type=jnp.float32
                )
                s = following

        def step(t, carry, tile=tile, p0=p0, low_last=low_last):
            k0 = anchor + t * TK
            clear = (k0 >= low_last) & (k0 + TK - 1 <= p0)

            @pl.when(clear)
            def _():
                tile(t, False)

            @pl.when(jnp.logical_not(clear))
            def _():
                tile(t, True)

            return carry

        lax.fori_loop((low_first - anchor) // TK, (p0 + TQ - 1 - anchor) // TK + 1, step, 0)
        side = tq * TQ // per_dev
        r0 = tq * TQ % per_dev
        parts = [(acc_ref[h] / l_ref[h]).T.astype(jnp.bfloat16) for h in range(GROUP)]

        def put(ref, c0, r0=r0, parts=parts):
            for h in range(GROUP):
                ref[r0 : r0 + TQ, c0 + h * HEAD_SIZE : c0 + (h + 1) * HEAD_SIZE] = parts[h]

        @pl.when(core == side)
        def _(put=put, side=side):
            put(own_out, side * GROUP * HEAD_SIZE)

        @pl.when(core != side)
        def _(put=put):
            put(send_out, 0)


def on_device(events, destination, segment, w_query, key_weight, value_weight):
    rows, width = events.shape
    ndev = lax.axis_size("ctx")
    me = lax.axis_index("ctx").astype(jnp.int32)
    core = me % 2
    chip_y = me // 2 % 4
    chip_x = me // 8
    half = GROUP * HEAD_SIZE
    shard = jax.ShapeDtypeStruct((rows + META, 2 * HEAD_SIZE), jnp.bfloat16)
    smem = pl.BlockSpec(memory_space=SMEM)
    vmem = pl.BlockSpec(memory_space=VMEM)
    hbm = pl.BlockSpec(memory_space=pl.ANY)

    def pairs(dx, dy, dc):
        return [
            (x * 8 + y * 2 + c, (x + dx) % 2 * 8 + (y + dy) % 4 * 2 + (c + dc) % 2)
            for x in range(2)
            for y in range(4)
            for c in range(2)
        ]

    up = lambda a: lax.ppermute(a, "ctx", pairs(0, 1, 0))
    down = lambda a: lax.ppermute(a, "ctx", pairs(0, -1, 0))
    across = lambda a: lax.ppermute(a, "ctx", pairs(1, 0, 0))
    swap = lambda a: lax.ppermute(a, "ctx", pairs(0, 0, 1))

    own, other = pl.pallas_call(
        kv_kernel,
        out_shape=(jax.ShapeDtypeStruct((2 * (rows + META), 2 * HEAD_SIZE), jnp.bfloat16), shard),
        in_specs=[smem, smem, smem, vmem, vmem, vmem],
        out_specs=(vmem, vmem),
        name="kv_projection",
    )(core[None], destination, segment, events, key_weight, value_weight)
    theirs = swap(other)
    q_send = pl.pallas_call(
        q_kernel,
        out_shape=jax.ShapeDtypeStruct((ndev, 2, BLK, half), jnp.bfloat16),
        in_specs=[smem, vmem, vmem, hbm],
        out_specs=hbm,
        scratch_shapes=[VMEM((2, rows, half), jnp.bfloat16), pltpu.SemaphoreType.DMA((rows // BLK * 2,))],
        name="query_projection",
    )(destination, events, w_query, own)
    mine = lax.dynamic_update_slice(own, theirs, (rows + META, 0))
    q_got = lax.all_to_all(q_send, "ctx", split_axis=0, concat_axis=0, tiled=True)
    y_down = up(mine)
    y_up = down(mine)
    x_far = across(mine)
    xd = up(x_far)
    y_two = down(y_up)
    xu = across(y_up)
    x_two = lax.ppermute(x_far, "ctx", pairs(0, 2, 0))
    out_half = jax.ShapeDtypeStruct((rows, half), jnp.bfloat16)
    mine_out, give_out = pl.pallas_call(
        attention_kernel,
        out_shape=(jax.ShapeDtypeStruct((rows, width), jnp.bfloat16), out_half),
        in_specs=[smem] + [hbm] * 9,
        out_specs=(vmem, vmem),
        scratch_shapes=[
            VMEM((ndev * rows + TK, 2 * HEAD_SIZE), jnp.bfloat16),
            VMEM((ndev * rows // TK + 1, HEAD_SIZE, TK), jnp.bfloat16),
            VMEM((2 * rows, half), jnp.bfloat16),
            VMEM((GROUP, 2 * HEAD_SIZE, TQ), jnp.bfloat16),
            VMEM((16, META, 2 * HEAD_SIZE), jnp.bfloat16),
            VMEM((16, HEAD_SIZE), jnp.int32),
            SMEM((16, HEAD_SIZE), jnp.int32),
            VMEM((GROUP, 1, TQ), jnp.float32),
            VMEM((GROUP, 1, TQ), jnp.float32),
            VMEM((GROUP, HEAD_SIZE, TQ), jnp.float32),
            pltpu.SemaphoreType.DMA((2,)),
            pltpu.SemaphoreType.DMA((16,)),
        ],
        name="attention",
    )(
        jnp.stack([chip_x, chip_y, core]),
        mine, y_down, y_up, x_far, xd, y_two, xu, x_two, q_got,
    )
    got = swap(give_out)
    return lax.dynamic_update_slice(mine_out, got, (jnp.int32(0), (1 - core) * half))


def solution(mesh):
    return jax.shard_map(
        on_device,
        mesh=mesh,
        in_specs=(P(("dp", "ctx"), None), P(("dp", "ctx")), P(("dp", "ctx")), P(), P(), P()),
        out_specs=P(("dp", "ctx"), None),
        check_vma=False,
    )
```

time: 349 us -> 137 us (0.39)
  the two profiles are of different devices: /device:TPU:1 before, /device:TPU:19 now
where the time goes in v1:
time: 137 us
  Pallas kernels  60.4 us (44%)
  waiting for transfers between devices  57.9 us (42%)
  starting transfers between devices  15.7 us (11%)
  local copies, waits for them, and re-layouts  2.2 us (2%)
    pallas_call x1, Pallas kernels, on_device(): pl.pallas_call(attention_kernel, out_shape=(jax.ShapeDtypeStruct((rows, w...  52.8 us
    ppermute x2, waiting for transfers between devices, on_device(): across = lambda a: lax.ppermute(a, 'ctx', pairs(1, 0, 0))  32.9 us
    ppermute x2, waiting for transfers between devices, on_device(): up = lambda a: lax.ppermute(a, 'ctx', pairs(0, 1, 0))  12.8 us
    ppermute x1, waiting for transfers between devices, on_device(): x_two = lax.ppermute(x_far, 'ctx', pairs(0, 2, 0))  8.35 us
    all_to_all x1, starting transfers between devices, on_device(): lax.all_to_all(q_send, 'ctx', split_axis=0, concat_axis=0, tiled=True)  6.17 us
    ppermute x2, starting transfers between devices, on_device(): up = lambda a: lax.ppermute(a, 'ctx', pairs(0, 1, 0))  5.31 us
    pallas_call x1, Pallas kernels, on_device(): pl.pallas_call(q_kernel, out_shape=jax.ShapeDtypeStruct((ndev, 2, BLK, ha...  4.32 us
    pallas_call x1, Pallas kernels, on_device(): pl.pallas_call(kv_kernel, out_shape=(jax.ShapeDtypeStruct((2 * (rows + ME...  3.32 us
  transfers between devices with their start and end apart: 10, of which 6 were waited for; matrix products, arithmetic and copies ran while one was open for 0% of the time, Pallas kernels for 0%

profile of v1, /device:TPU:19, one launch (start us, length us, event | category | flops | bytes accessed | tf_op | source)
XLA Modules:
  0.0 136.9 jit_solution(5578549082572664212)
XLA Ops:
  0.0 3.3 %kv_projection.1 = (bf16[1056,256]{1,0:T(8,128)(2,1)}, bf16[528,256]{1,0:T(8,128)(2,1)}) custom-call(s32[1]{0:T(128)} %bitcast.2.core_ref, s32[512]{0:T(512)} %dest_ref.3, s32[512]{0:T(512)} %seg_ref.1, bf16[512,1024]{1,0:T(8,128)(2,1)} %ev_ref.3, bf16[1024,256]{1,0:T(8,128)(2,1)} %kw_ref.1, bf16[1024,256]{1,0:T(8,128)(2,1)} %vw_ref.1), custom_call_target="tpu_custom_call" | custom-call | tf_op jit(solution)/shard_map/kv_projection/pallas_call | solution.py:280
  3.3 4.3 %query_projection.1 = bf16[16,2,64,512]{3,2,1,0:T(8,128)(2,1)} custom-call(s32[512]{0:T(512)} %dest_ref.3, bf16[512,1024]{1,0:T(8,128)(2,1)} %ev_ref.3, bf16[1024,1024]{1,0:T(8,128)(2,1)} %wq_ref.1, bf16[1056,256]{1,0:T(8,128)(2,1)} %get-tuple-element.9.after_ref), custom_call_target="tpu_custom_call" | custom-call | tf_op jit(solution)/shard_map/query_projection/pallas_call | solution.py:288
  7.7 0.0 copy-start.4
  7.7 0.0 copy-start.1
  7.7 6.2 %all-to-all-start = ((bf16[16,2,64,512]{3,2,1,0:T(8,128)(2,1)}), bf16[16,2,64,512]{3,2,1,0:T(8,128)(2,1)S(1)}, u32[]{:S(2)}, u32[]{:S(2)}) async-start(bf16[16,2,64,512]{3,2,1,0:T(8,128)(2,1)} %query_projection.1), calls=%async_computation | async-start | bytes 4194304 | tf_op jit(solution)/shard_map/all_to_all | solution.py:297
  13.8 0.0 copy-done.4
  13.8 0.5 collective-permute-start
  14.3 1.3 collective-permute-done
  15.7 0.0 copy-done.1
  15.7 0.0 copy-start.2
  15.7 0.4 collective-permute-start.3
  16.1 0.3 collective-permute-start.2
  16.3 1.2 collective-permute-start.1
  17.5 32.9 %collective-permute-done.3.refs_3_ = bf16[1056,256]{1,0:T(8,128)(2,1)S(1)} collective-permute-done((bf16[1056,256]{1,0:T(8,128)(2,1)S(1)}, bf16[1056,256]{1,0:T(8,128)(2,1)S(1)}, u32[]{:S(2)}, u32[]{:S(2)}) %collective-permute-start.3) | collective-permute-done | bytes 540704 | tf_op jit(solution)/shard_map/ppermute | solution.py:277
  50.4 0.7 collective-permute-start.7
  51.1 4.1 %collective-permute-start.4 = (bf16[1056,256]{1,0:T(8,128)(2,1)S(1)}, bf16[1056,256]{1,0:T(8,128)(2,1)}, u32[]{:S(2)}, u32[]{:S(2)}) collective-permute-start(bf16[1056,256]{1,0:T(8,128)(2,1)S(1)} %collective-permute-done.3.refs_3_), channel_id=1, source_target_pairs={{0,2},{1,3},{2,4},{3,5},{4,6},{5,7},{6,0},{7,1},{8,10},{9,11},{10,... | collective-permute-start | bytes 1622024 | tf_op jit(solution)/shard_map/ppermute | solution.py:275
  55.2 0.0 collective-permute-done.2.refs_2_
  55.2 0.8 collective-permute-start.6
  56.0 0.0 collective-permute-start.5
  56.0 0.6 pad_add_fusion.where_ref
  56.6 0.0 collective-permute-done.1.refs_1_
  56.6 8.3 %collective-permute-done.7.refs_7_ = bf16[1056,256]{1,0:T(8,128)(2,1)} collective-permute-done((bf16[1056,256]{1,0:T(8,128)(2,1)S(1)}, bf16[1056,256]{1,0:T(8,128)(2,1)}, u32[]{:S(2)}, u32[]{:S(2)}) %collective-permute-start.7) | collective-permute-done | bytes 540704 | tf_op jit(solution)/shard_map/ppermute | solution.py:304
  65.0 12.8 %collective-permute-done.4.refs_4_ = bf16[1056,256]{1,0:T(8,128)(2,1)} collective-permute-done((bf16[1056,256]{1,0:T(8,128)(2,1)S(1)}, bf16[1056,256]{1,0:T(8,128)(2,1)}, u32[]{:S(2)}, u32[]{:S(2)}) %collective-permute-start.4) | collective-permute-done | bytes 540704 | tf_op jit(solution)/shard_map/ppermute | solution.py:275
  77.8 0.0 collective-permute-done.6.refs_6_
  77.8 0.8 collective-permute-done.5.refs_5_
  78.6 0.0 all-to-all-done.refs_8_
  78.6 0.0 copy-done.2
  78.6 1.3 copy-done
  80.0 52.8 %attention.1 = (bf16[512,1024]{1,0:T(8,128)(2,1)}, bf16[512,512]{1,0:T(8,128)(2,1)}) custom-call(s32[3]{0:T(128)} %pad_add_fusion.where_ref, bf16[1056,256]{1,0:T(8,128)(2,1)} %copy-done.2, bf16[1056,256]{1,0:T(8,128)(2,1)} %collective-permute-done.1.refs_1_, bf16[1056,256]{1,0:T(8,128)(2,1)} %collective-permute-done.2.refs_2_, bf16[1056,256]{1,0:T(8,128)(2,1)} %copy-done.3, ...), custom_call_target="tpu_custom_call" | custom-call | tf_op jit(solution)/shard_map/attention/pallas_call | solution.py:306
  132.7 1.6 %collective-permute-start.8 = (bf16[512,512]{1,0:T(8,128)(2,1)}, bf16[512,512]{1,0:T(8,128)(2,1)S(1)}, u32[]{:S(2)}, u32[]{:S(2)}) collective-permute-start(bf16[512,512]{1,0:T(8,128)(2,1)} %get-tuple-element.12), channel_id=1, source_target_pairs={{0,1},{1,0},{2,3},{3,2},{4,5},{5,4},{6,7},{7,6},{8,9},{9,8},{10,11... | collective-permute-start | bytes 1572872 | tf_op jit(solution)/shard_map/ppermute | solution.py:278
  134.3 1.7 %collective-permute-done.8 = bf16[512,512]{1,0:T(8,128)(2,1)S(1)} collective-permute-done((bf16[512,512]{1,0:T(8,128)(2,1)}, bf16[512,512]{1,0:T(8,128)(2,1)S(1)}, u32[]{:S(2)}, u32[]{:S(2)}) %collective-permute-start.8) | collective-permute-done | bytes 524320 | tf_op jit(solution)/shard_map/ppermute | solution.py:278
  136.1 0.8 constant_dynamic-update-slice_fusion.1
  (4 shorter events, 0.0 us)
Async XLA Ops:
  7.7 6.2 %copy-start.4 = (bf16[528,256]{1,0:T(8,128)(2,1)S(1)}, bf16[528,256]{1,0:T(8,128)(2,1)}, u32[]{:S(2)}) copy-start(bf16[528,256]{1,0:T(8,128)(2,1)} %get-tuple-element.10) | copy-start | bytes 811012
  7.7 8.0 %copy-start.1 = (bf16[1056,256]{1,0:T(8,128)(2,1)S(1)}, bf16[1056,256]{1,0:T(8,128)(2,1)}, u32[]{:S(2)}) copy-start(bf16[1056,256]{1,0:T(8,128)(2,1)} %get-tuple-element.9.after_ref) | copy-start | bytes 1622020
  7.7 70.9 %all-to-all-start = ((bf16[16,2,64,512]{3,2,1,0:T(8,128)(2,1)}), bf16[16,2,64,512]{3,2,1,0:T(8,128)(2,1)S(1)}, u32[]{:S(2)}, u32[]{:S(2)}) async-start(bf16[16,2,64,512]{3,2,1,0:T(8,128)(2,1)} %query_projection.1), calls=%async_computation | async-start | bytes 4194304 | tf_op jit(solution)/shard_map/all_to_all | solution.py:297
  13.8 1.8 %collective-permute-start = (bf16[528,256]{1,0:T(8,128)(2,1)S(1)}, bf16[528,256]{1,0:T(8,128)(2,1)S(1)}, u32[]{:S(2)}, u32[]{:S(2)}) collective-permute-start(bf16[528,256]{1,0:T(8,128)(2,1)S(1)} %copy-done.4), channel_id=1, source_target_pairs={{0,1},{1,0},{2,3},{3,2},{4,5},{5,4},{6,7},{7,6},{8,9},{9,8},{10,11... | collective-permute-start | bytes 811016 | tf_op jit(solution)/shard_map/ppermute | solution.py:278
  15.7 62.9 %copy-start.2 = (bf16[1056,256]{1,0:T(8,128)(2,1)}, bf16[1056,256]{1,0:T(8,128)(2,1)S(1)}, u32[]{:S(2)}) copy-start(bf16[1056,256]{1,0:T(8,128)(2,1)S(1)} %constant_dynamic-update-slice_fusion.refs_0_) | copy-start | bytes 1622020
  15.7 34.7 %collective-permute-start.3 = (bf16[1056,256]{1,0:T(8,128)(2,1)S(1)}, bf16[1056,256]{1,0:T(8,128)(2,1)S(1)}, u32[]{:S(2)}, u32[]{:S(2)}) collective-permute-start(bf16[1056,256]{1,0:T(8,128)(2,1)S(1)} %constant_dynamic-update-slice_fusion.refs_0_), channel_id=1, source_target_pairs={{0,8},{1,9},{2,10},{3,11},{4,12},{5,13},{6,14},{7,15},{8,0},{9,1},... | collective-permute-start | bytes 1622024 | tf_op jit(solution)/shard_map/ppermute | solution.py:277
  16.1 39.1 %collective-permute-start.2 = (bf16[1056,256]{1,0:T(8,128)(2,1)S(1)}, bf16[1056,256]{1,0:T(8,128)(2,1)}, u32[]{:S(2)}, u32[]{:S(2)}) collective-permute-start(bf16[1056,256]{1,0:T(8,128)(2,1)S(1)} %constant_dynamic-update-slice_fusion.refs_0_), channel_id=1, source_target_pairs={{0,6},{1,7},{2,0},{3,1},{4,2},{5,3},{6,4},{7,5},{8,14},{9,15},{10,... | collective-permute-start | bytes 1622024 | tf_op jit(solution)/shard_map/ppermute | solution.py:276
  16.3 40.3 %collective-permute-start.1 = (bf16[1056,256]{1,0:T(8,128)(2,1)S(1)}, bf16[1056,256]{1,0:T(8,128)(2,1)}, u32[]{:S(2)}, u32[]{:S(2)}) collective-permute-start(bf16[1056,256]{1,0:T(8,128)(2,1)S(1)} %constant_dynamic-update-slice_fusion.refs_0_), channel_id=1, source_target_pairs={{0,2},{1,3},{2,4},{3,5},{4,6},{5,7},{6,0},{7,1},{8,10},{9,11},{10,... | collective-permute-start | bytes 1622024 | tf_op jit(solution)/shard_map/ppermute | solution.py:275
  50.4 28.2 %copy-start.3 = (bf16[1056,256]{1,0:T(8,128)(2,1)}, bf16[1056,256]{1,0:T(8,128)(2,1)S(1)}, u32[]{:S(2)}) copy-start(bf16[1056,256]{1,0:T(8,128)(2,1)S(1)} %collective-permute-done.3.refs_3_) | copy-start | bytes 1622020
  50.4 14.6 %collective-permute-start.7 = (bf16[1056,256]{1,0:T(8,128)(2,1)S(1)}, bf16[1056,256]{1,0:T(8,128)(2,1)}, u32[]{:S(2)}, u32[]{:S(2)}) collective-permute-start(bf16[1056,256]{1,0:T(8,128)(2,1)S(1)} %collective-permute-done.3.refs_3_), channel_id=1, source_target_pairs={{0,4},{1,5},{2,6},{3,7},{4,0},{5,1},{6,2},{7,3},{8,12},{9,13},{10,... | collective-permute-start | bytes 1622024 | tf_op jit(solution)/shard_map/ppermute | solution.py:304
  51.1 26.7 %collective-permute-start.4 = (bf16[1056,256]{1,0:T(8,128)(2,1)S(1)}, bf16[1056,256]{1,0:T(8,128)(2,1)}, u32[]{:S(2)}, u32[]{:S(2)}) collective-permute-start(bf16[1056,256]{1,0:T(8,128)(2,1)S(1)} %collective-permute-done.3.refs_3_), channel_id=1, source_target_pairs={{0,2},{1,3},{2,4},{3,5},{4,6},{5,7},{6,0},{7,1},{8,10},{9,11},{10,... | collective-permute-start | bytes 1622024 | tf_op jit(solution)/shard_map/ppermute | solution.py:275
  55.2 22.6 %collective-permute-start.6 = (bf16[1056,256]{1,0:T(8,128)(2,1)}, bf16[1056,256]{1,0:T(8,128)(2,1)}, u32[]{:S(2)}, u32[]{:S(2)}) collective-permute-start(bf16[1056,256]{1,0:T(8,128)(2,1)} %collective-permute-done.2.refs_2_), channel_id=1, source_target_pairs={{0,8},{1,9},{2,10},{3,11},{4,12},{5,13},{6,14},{7,15},{8,0},{9,1},... | collective-permute-start | bytes 1622024 | tf_op jit(solution)/shard_map/ppermute | solution.py:277
  56.0 22.6 %collective-permute-start.5 = (bf16[1056,256]{1,0:T(8,128)(2,1)}, bf16[1056,256]{1,0:T(8,128)(2,1)}, u32[]{:S(2)}, u32[]{:S(2)}) collective-permute-start(bf16[1056,256]{1,0:T(8,128)(2,1)} %collective-permute-done.2.refs_2_), channel_id=1, source_target_pairs={{0,6},{1,7},{2,0},{3,1},{4,2},{5,3},{6,4},{7,5},{8,14},{9,15},{10,... | collective-permute-start | bytes 1622024 | tf_op jit(solution)/shard_map/ppermute | solution.py:276
  78.6 1.3 copy-start
  132.7 3.4 %collective-permute-start.8 = (bf16[512,512]{1,0:T(8,128)(2,1)}, bf16[512,512]{1,0:T(8,128)(2,1)S(1)}, u32[]{:S(2)}, u32[]{:S(2)}) collective-permute-start(bf16[512,512]{1,0:T(8,128)(2,1)} %get-tuple-element.12), channel_id=1, source_target_pairs={{0,1},{1,0},{2,3},{3,2},{4,5},{5,4},{6,7},{7,6},{8,9},{9,8},{10,11... | collective-permute-start | bytes 1572872 | tf_op jit(solution)/shard_map/ppermute | solution.py:278

commit v2 on v1

--- a/solution.py
+++ b/solution.py
@@ -100,8 +100,8 @@
 
 def attention_kernel(where_ref, *refs):
     shards = refs[:8]
-    q_in_ref, own_out, send_out = refs[8:11]
-    kv, v_t, q_buf, q_t, meta_bf, meta_int, table, m_ref, l_ref, acc_ref, sem, meta_sem = refs[11:]
+    last_ref, q_in_ref, own_out, send_out = refs[8:12]
+    kv, v_t, q_buf, q_t, meta_bf, meta_int, table, origin, m_ref, l_ref, acc_ref, sem, meta_sem = refs[12:]
     chip_x, chip_y, core = where_ref[0], where_ref[1], where_ref[2]
     per_dev = (kv.shape[0] - TK) // 16
     shard_rows = per_dev + META
@@ -109,7 +109,9 @@
     offsets = [(0, 0), (0, 3), (0, 1), (1, 0), (1, 3), (0, 2), (1, 1), (1, 2)]
 
     def source(i, h):
-        return shards[i], h * shard_rows
+        if i < 7:
+            return shards[i], h * shard_rows
+        return (shards[7], 0) if h == 0 else (last_ref, 0)
 
     fetches = []
     for i in range(8):
@@ -143,16 +145,19 @@
                     ref.at[pl.ds(base + b * BLK, BLK), :], kv.at[pl.ds(j * BLK, BLK), :], sem.at[0]
                 ).start()
 
-                @pl.when(j // (2 * blocks) == my_chip)
-                def _():
-                    local = j - my_chip * 2 * blocks
-                    pltpu.make_async_copy(
-                        q_in_ref.at[device, local // blocks], q_buf.at[pl.ds(local * BLK, BLK), :], sem.at[1]
-                    ).start()
-
+                origin[j] = device
                 return carry
 
-            lax.fori_loop(0, blocks, place, 0)
+            lax.fori_loop(0, blocks, place, 0, unroll=True)
+    q_copies = []
+    for n in range(2 * blocks):
+        copy = pltpu.make_async_copy(
+            q_in_ref.at[origin[my_chip * 2 * blocks + n], n // blocks],
+            q_buf.at[n * BLK : (n + 1) * BLK, :],
+            meta_sem.at[n],
+        )
+        copy.start()
+        q_copies.append(copy)
     bound = [table[0, 16 + 2 * s] + table[0, 17 + 2 * s] for s in range(3)]
 
     def start_of(pos):
@@ -163,12 +168,24 @@
 
     rows_all = pl.ds(0, 16 * per_dev)
     kv[16 * per_dev :, :] = jnp.zeros((TK, 2 * HEAD_SIZE), jnp.bfloat16)
-    pltpu.make_async_copy(kv.at[rows_all], kv.at[rows_all], sem.at[0]).wait()
-    pltpu.make_async_copy(q_buf, q_buf, sem.at[1]).wait()
 
     chip_rows = 2 * per_dev
     first = my_chip * chip_rows
     anchor = start_of(first) // BLK * BLK
+
+    for copy in q_copies:
+        copy.wait()
+    units = [(tq, h) for tq in range(chip_rows // TQ) for h in range(GROUP)]
+    for u, (tq, h) in enumerate(units):
+        q = q_buf[tq * TQ : (tq + 1) * TQ, h * HEAD_SIZE : (h + 1) * HEAD_SIZE]
+        q = q.astype(jnp.float32) * SCALE2
+        high = q.astype(jnp.bfloat16)
+        q_t[u, :HEAD_SIZE] = high.T
+        q_t[u, HEAD_SIZE:] = (q - high.astype(jnp.float32)).astype(jnp.bfloat16).T
+        m_ref[u] = jnp.full((1, TQ), NEGATIVE_FILL, jnp.float32)
+        l_ref[u] = jnp.zeros((1, TQ), jnp.float32)
+        acc_ref[u] = jnp.zeros((HEAD_SIZE, TQ), jnp.float32)
+    pltpu.make_async_copy(kv.at[rows_all], kv.at[rows_all], sem.at[0]).wait()
 
     def turn(t, carry):
         rows = pl.ds(pl.multiple_of(anchor + t * TK, BLK), TK)
@@ -177,66 +194,66 @@
 
     lax.fori_loop(0, (first + chip_rows - anchor + TK - 1) // TK, turn, 0)
 
+    low_last = start_of(first + chip_rows - 1)
+
+    def attend(work, k, v, allowed):
+        def score(u):
+            s = jnp.dot(k, q_t[u], preferred_element_type=jnp.float32)
+            return s if allowed is None else jnp.where(allowed, s, NEGATIVE_FILL)
+
+        s = score(work[0])
+        for n, u in enumerate(work):
+            following = score(work[n + 1]) if n + 1 < len(work) else None
+            m_old = m_ref[u]
+            m_new = jnp.maximum(m_old, jnp.max(s, axis=0, keepdims=True))
+            p = jnp.exp2(s - m_new)
+            shrink = jnp.exp2(m_old - m_new)
+            m_ref[u] = m_new
+            l_ref[u] = l_ref[u] * shrink + jnp.sum(p, axis=0, keepdims=True)
+            acc_ref[u] = acc_ref[u] * shrink + jnp.dot(
+                v, p.astype(jnp.bfloat16), preferred_element_type=jnp.float32
+            )
+            s = following
+
+    def keys_at(k0, count):
+        k = kv[pl.ds(k0, count), :HEAD_SIZE]
+        return jnp.concatenate([k, k], axis=1)
+
+    def step(t, carry):
+        k0 = pl.multiple_of(anchor + t * TK, BLK)
+        clear = (k0 >= low_last) & (k0 + TK - 1 <= first)
+
+        @pl.when(clear)
+        def _():
+            attend(range(len(units)), keys_at(k0, TK), v_t[t], None)
+
+        for tq in range(chip_rows // TQ):
+            for piece in range(TK // TQ):
+                p0 = first + tq * TQ
+                from_key = pl.multiple_of(k0 + piece * TQ, BLK)
+                used = (from_key <= p0 + TQ - 1) & (from_key + TQ - 1 >= start_of(p0))
+
+                @pl.when(jnp.logical_not(clear) & used)
+                def _(tq=tq, piece=piece, p0=p0, from_key=from_key):
+                    kpos = from_key + lax.broadcasted_iota(jnp.int32, (TQ, TQ), 0)
+                    qpos = p0 + lax.broadcasted_iota(jnp.int32, (1, TQ), 1)
+                    allowed = (kpos <= qpos) & (kpos >= start_of(qpos))
+                    attend(
+                        [tq * GROUP + h for h in range(GROUP)],
+                        keys_at(from_key, TQ),
+                        v_t[t, :, piece * TQ : (piece + 1) * TQ],
+                        allowed,
+                    )
+
+        return carry
+
+    lax.fori_loop(0, (first + chip_rows - anchor + TK - 1) // TK, step, 0)
     for tq in range(chip_rows // TQ):
-        p0 = first + tq * TQ
-        low_first = start_of(p0)
-        low_last = start_of(p0 + TQ - 1)
-        for h in range(GROUP):
-            q = q_buf[tq * TQ : (tq + 1) * TQ, h * HEAD_SIZE : (h + 1) * HEAD_SIZE]
-            q = q.astype(jnp.float32) * SCALE2
-            high = q.astype(jnp.bfloat16)
-            q_t[h, :HEAD_SIZE] = high.T
-            q_t[h, HEAD_SIZE:] = (q - high.astype(jnp.float32)).astype(jnp.bfloat16).T
-            m_ref[h] = jnp.full((1, TQ), NEGATIVE_FILL, jnp.float32)
-            l_ref[h] = jnp.zeros((1, TQ), jnp.float32)
-            acc_ref[h] = jnp.zeros((HEAD_SIZE, TQ), jnp.float32)
-
-        def tile(t, masked, p0=p0):
-            k0 = pl.multiple_of(anchor + t * TK, BLK)
-            k = kv[pl.ds(k0, TK), :HEAD_SIZE]
-            k = jnp.concatenate([k, k], axis=1)
-            v = v_t[t]
-            if masked:
-                kpos = k0 + lax.broadcasted_iota(jnp.int32, (TK, TQ), 0)
-                qpos = p0 + lax.broadcasted_iota(jnp.int32, (1, TQ), 1)
-                allowed = (kpos <= qpos) & (kpos >= start_of(qpos))
-
-            def score(h):
-                s = jnp.dot(k, q_t[h], preferred_element_type=jnp.float32)
-                return jnp.where(allowed, s, NEGATIVE_FILL) if masked else s
-
-            s = score(0)
-            for h in range(GROUP):
-                following = score(h + 1) if h + 1 < GROUP else None
-                m_old = m_ref[h]
-                m_new = jnp.maximum(m_old, jnp.max(s, axis=0, keepdims=True))
-                p = jnp.exp2(s - m_new)
-                shrink = jnp.exp2(m_old - m_new)
-                m_ref[h] = m_new
-                l_ref[h] = l_ref[h] * shrink + jnp.sum(p, axis=0, keepdims=True)
-                acc_ref[h] = acc_ref[h] * shrink + jnp.dot(
-                    v, p.astype(jnp.bfloat16), preferred_element_type=jnp.float32
-                )
-                s = following
-
-        def step(t, carry, tile=tile, p0=p0, low_last=low_last):
-            k0 = anchor + t * TK
-            clear = (k0 >= low_last) & (k0 + TK - 1 <= p0)
-
-            @pl.when(clear)
-            def _():
-                tile(t, False)
-
-            @pl.when(jnp.logical_not(clear))
-            def _():
-                tile(t, True)
-
-            return carry
-
-        lax.fori_loop((low_first - anchor) // TK, (p0 + TQ - 1 - anchor) // TK + 1, step, 0)
         side = tq * TQ // per_dev
         r0 = tq * TQ % per_dev
-        parts = [(acc_ref[h] / l_ref[h]).T.astype(jnp.bfloat16) for h in range(GROUP)]
+        parts = [
+            (acc_ref[tq * GROUP + h] / l_ref[tq * GROUP + h]).astype(jnp.bfloat16).T for h in range(GROUP)
+        ]
 
         def put(ref, c0, r0=r0, parts=parts):
             for h in range(GROUP):
@@ -295,37 +312,41 @@
     )(destination, events, w_query, own)
     mine = lax.dynamic_update_slice(own, theirs, (rows + META, 0))
     q_got = lax.all_to_all(q_send, "ctx", split_axis=0, concat_axis=0, tiled=True)
+    shard_rows = rows + META
     y_down = up(mine)
     y_up = down(mine)
     x_far = across(mine)
     xd = up(x_far)
     y_two = down(y_up)
     xu = across(y_up)
-    x_two = lax.ppermute(x_far, "ctx", pairs(0, 2, 0))
+    x_two_a = up(xd[:shard_rows])
+    x_two_b = across(y_two[shard_rows:])
+    units = 2 * rows // TQ * GROUP
     out_half = jax.ShapeDtypeStruct((rows, half), jnp.bfloat16)
     mine_out, give_out = pl.pallas_call(
         attention_kernel,
         out_shape=(jax.ShapeDtypeStruct((rows, width), jnp.bfloat16), out_half),
-        in_specs=[smem] + [hbm] * 9,
+        in_specs=[smem] + [hbm] * 10,
         out_specs=(vmem, vmem),
         scratch_shapes=[
             VMEM((ndev * rows + TK, 2 * HEAD_SIZE), jnp.bfloat16),
             VMEM((ndev * rows // TK + 1, HEAD_SIZE, TK), jnp.bfloat16),
             VMEM((2 * rows, half), jnp.bfloat16),
-            VMEM((GROUP, 2 * HEAD_SIZE, TQ), jnp.bfloat16),
+            VMEM((units, 2 * HEAD_SIZE, TQ), jnp.bfloat16),
             VMEM((16, META, 2 * HEAD_SIZE), jnp.bfloat16),
             VMEM((16, HEAD_SIZE), jnp.int32),
             SMEM((16, HEAD_SIZE), jnp.int32),
-            VMEM((GROUP, 1, TQ), jnp.float32),
-            VMEM((GROUP, 1, TQ), jnp.float32),
-            VMEM((GROUP, HEAD_SIZE, TQ), jnp.float32),
-            pltpu.SemaphoreType.DMA((2,)),
+            SMEM((ndev * rows // BLK,), jnp.int32),
+            VMEM((units, 1, TQ), jnp.float32),
+            VMEM((units, 1, TQ), jnp.float32),
+            VMEM((units, HEAD_SIZE, TQ), jnp.float32),
+            pltpu.SemaphoreType.DMA((1,)),
             pltpu.SemaphoreType.DMA((16,)),
         ],
         name="attention",
     )(
         jnp.stack([chip_x, chip_y, core]),
-        mine, y_down, y_up, x_far, xd, y_two, xu, x_two, q_got,
+        mine, y_down, y_up, x_far, xd, y_two, xu, x_two_a, x_two_b, q_got,
     )
     got = swap(give_out)
     return lax.dynamic_update_slice(mine_out, got, (jnp.int32(0), (1 - core) * half))

time: 137 us -> 148 us (1.080)
  the two profiles are of different devices: /device:TPU:19 before, /device:TPU:51 now
where the time goes in v2:
time: 148 us; the launch traced here: 147 us
  Pallas kernels  66.3 us (45%)
  waiting for transfers between devices  61.6 us (42%)
  starting transfers between devices  13.4 us (9%)
  local copies, waits for them, and re-layouts  5.17 us (3%)
    pallas_call x1, Pallas kernels, on_device(): pl.pallas_call(attention_kernel, out_shape=(jax.ShapeDtypeStruct((rows, w...  58.7 us
    ppermute x3, waiting for transfers between devices, on_device(): across = lambda a: lax.ppermute(a, 'ctx', pairs(1, 0, 0))  34 us
    ppermute x3, waiting for transfers between devices, on_device(): up = lambda a: lax.ppermute(a, 'ctx', pairs(0, 1, 0))  24.5 us
    all_to_all x1, starting transfers between devices, on_device(): lax.all_to_all(q_send, 'ctx', split_axis=0, concat_axis=0, tiled=True)  6.11 us
    pallas_call x1, Pallas kernels, on_device(): pl.pallas_call(q_kernel, out_shape=jax.ShapeDtypeStruct((ndev, 2, BLK, ha...  4.32 us
    pallas_call x1, Pallas kernels, on_device(): pl.pallas_call(kv_kernel, out_shape=(jax.ShapeDtypeStruct((2 * (rows + ME...  3.33 us
    ppermute x2, waiting for transfers between devices, on_device(): swap = lambda a: lax.ppermute(a, 'ctx', pairs(0, 0, 1))  3.09 us
    ppermute x2, starting transfers between devices, on_device(): down = lambda a: lax.ppermute(a, 'ctx', pairs(0, -1, 0))  3.06 us
  transfers between devices with their start and end apart: 11, of which 6 were waited for; matrix products, arithmetic and copies ran while one was open for 1% of the time, Pallas kernels for 0%

profile of v2, /device:TPU:51, one launch (start us, length us, event | category | flops | bytes accessed | tf_op | source)
XLA Modules:
  0.0 147.3 jit_solution(5450086440829885697)
XLA Ops:
  0.0 3.3 %kv_projection.1 = (bf16[1056,256]{1,0:T(8,128)(2,1)}, bf16[528,256]{1,0:T(8,128)(2,1)}) custom-call(s32[1]{0:T(128)} %bitcast.2.core_ref, s32[512]{0:T(512)} %dest_ref.3, s32[512]{0:T(512)} %seg_ref.1, bf16[512,1024]{1,0:T(8,128)(2,1)} %ev_ref.3, bf16[1024,256]{1,0:T(8,128)(2,1)} %kw_ref.1, bf16[1024,256]{1,0:T(8,128)(2,1)} %vw_ref.1), custom_call_target="tpu_custom_call" | custom-call | tf_op jit(solution)/shard_map/kv_projection/pallas_call | solution.py:297
  3.3 4.3 %query_projection.1 = bf16[16,2,64,512]{3,2,1,0:T(8,128)(2,1)} custom-call(s32[512]{0:T(512)} %dest_ref.3, bf16[512,1024]{1,0:T(8,128)(2,1)} %ev_ref.3, bf16[1024,1024]{1,0:T(8,128)(2,1)} %wq_ref.1, bf16[1056,256]{1,0:T(8,128)(2,1)} %get-tuple-element.9.after_ref), custom_call_target="tpu_custom_call" | custom-call | tf_op jit(solution)/shard_map/query_projection/pallas_call | solution.py:305
  7.7 0.0 copy-start.1
  7.7 6.1 %all-to-all-start = ((bf16[16,2,64,512]{3,2,1,0:T(8,128)(2,1)}), bf16[16,2,64,512]{3,2,1,0:T(8,128)(2,1)S(1)}, u32[]{:S(2)}, u32[]{:S(2)}) async-start(bf16[16,2,64,512]{3,2,1,0:T(8,128)(2,1)} %query_projection.1), calls=%async_computation | async-start | bytes 4194304 | tf_op jit(solution)/shard_map/all_to_all | solution.py:314
  13.8 0.5 collective-permute-start
  14.3 1.3 collective-permute-done
  15.7 0.4 collective-permute-start.3
  16.0 0.3 collective-permute-start.2
  16.3 34.0 %collective-permute-done.3.refs_3_ = bf16[1056,256]{1,0:T(8,128)(2,1)S(1)} collective-permute-done((bf16[1056,256]{1,0:T(8,128)(2,1)S(1)}, bf16[1056,256]{1,0:T(8,128)(2,1)S(1)}, u32[]{:S(2)}, u32[]{:S(2)}) %collective-permute-start.3) | collective-permute-done | bytes 540704 | tf_op jit(solution)/shard_map/ppermute | solution.py:294
  50.3 0.2 collective-permute-start.4
  50.6 0.0 collective-permute-done.2.refs_2_
  50.6 2.8 %collective-permute-start.5 = (bf16[1056,256]{1,0:T(8,128)(2,1)}, bf16[1056,256]{1,0:T(8,128)(2,1)S(1)}, u32[]{:S(2)}, u32[]{:S(2)}) collective-permute-start(bf16[1056,256]{1,0:T(8,128)(2,1)} %collective-permute-done.2.refs_2_), channel_id=1, source_target_pairs={{0,6},{1,7},{2,0},{3,1},{4,2},{5,3},{6,4},{7,5},{8,14},{9,15},{10,... | collective-permute-start | bytes 1622024 | tf_op jit(solution)/shard_map/ppermute | solution.py:293
  53.4 0.8 collective-permute-start.6
  54.1 10.9 %collective-permute-done.4.refs_4_ = bf16[1056,256]{1,0:T(8,128)(2,1)S(1)} collective-permute-done((bf16[1056,256]{1,0:T(8,128)(2,1)S(1)}, bf16[1056,256]{1,0:T(8,128)(2,1)S(1)}, u32[]{:S(2)}, u32[]{:S(2)}) %collective-permute-start.4) | collective-permute-done | bytes 540704 | tf_op jit(solution)/shard_map/ppermute | solution.py:292
  65.1 0.8 slice.8
  65.8 0.0 collective-permute-start.7
  65.8 0.0 collective-permute-done.5.refs_5_
  65.8 0.8 copy-done.4
  66.6 0.7 slice.9
  67.4 0.8 collective-permute-start.8
  68.1 0.7 pad_add_fusion.where_ref
  68.8 7.9 %collective-permute-done.1.refs_1_ = bf16[1056,256]{1,0:T(8,128)(2,1)} collective-permute-done((bf16[1056,256]{1,0:T(8,128)(2,1)S(1)}, bf16[1056,256]{1,0:T(8,128)(2,1)}, u32[]{:S(2)}, u32[]{:S(2)}) %collective-permute-start.1) | collective-permute-done | bytes 540704 | tf_op jit(solution)/shard_map/ppermute | solution.py:292
  76.6 0.0 collective-permute-done.6.refs_6_
  76.6 5.7 %collective-permute-done.7.refs_7_ = bf16[528,256]{1,0:T(8,128)(2,1)S(1)} collective-permute-done((bf16[528,256]{1,0:T(8,128)(2,1)}, bf16[528,256]{1,0:T(8,128)(2,1)S(1)}, u32[]{:S(2)}, u32[]{:S(2)}) %collective-permute-start.7) | collective-permute-done | bytes 270368 | tf_op jit(solution)/shard_map/ppermute | solution.py:292
  82.3 0.0 collective-permute-done.8.refs_8_
  82.3 0.0 all-to-all-done.refs_9_
  82.4 0.7 copy-done.6
  83.1 1.3 copy-done
  84.4 58.7 %attention.1 = (bf16[512,1024]{1,0:T(8,128)(2,1)}, bf16[512,512]{1,0:T(8,128)(2,1)}) custom-call(s32[3]{0:T(128)} %pad_add_fusion.where_ref, bf16[1056,256]{1,0:T(8,128)(2,1)} %copy-done.2, bf16[1056,256]{1,0:T(8,128)(2,1)} %collective-permute-done.1.refs_1_, bf16[1056,256]{1,0:T(8,128)(2,1)} %collective-permute-done.2.refs_2_, bf16[1056,256]{1,0:T(8,128)(2,1)} %copy-done.5, ...), custom_call_target="tpu_custom_call" | custom-call | tf_op jit(solution)/shard_map/attention/pallas_call | solution.py:326
  143.1 1.6 %collective-permute-start.9 = (bf16[512,512]{1,0:T(8,128)(2,1)}, bf16[512,512]{1,0:T(8,128)(2,1)S(1)}, u32[]{:S(2)}, u32[]{:S(2)}) collective-permute-start(bf16[512,512]{1,0:T(8,128)(2,1)} %get-tuple-element.12), channel_id=1, source_target_pairs={{0,1},{1,0},{2,3},{3,2},{4,5},{5,4},{6,7},{7,6},{8,9},{9,8},{10,11... | collective-permute-start | bytes 1572872 | tf_op jit(solution)/shard_map/ppermute | solution.py:295
  144.7 1.7 %collective-permute-done.9 = bf16[512,512]{1,0:T(8,128)(2,1)S(1)} collective-permute-done((bf16[512,512]{1,0:T(8,128)(2,1)}, bf16[512,512]{1,0:T(8,128)(2,1)S(1)}, u32[]{:S(2)}, u32[]{:S(2)}) %collective-permute-start.9) | collective-permute-done | bytes 524320 | tf_op jit(solution)/shard_map/ppermute | solution.py:295
  146.5 0.8 constant_dynamic-update-slice_fusion.1
  (14 shorter events, 0.0 us)
Async XLA Ops:
  7.7 6.1 %copy-start.7 = (bf16[528,256]{1,0:T(8,128)(2,1)S(1)}, bf16[528,256]{1,0:T(8,128)(2,1)}, u32[]{:S(2)}) copy-start(bf16[528,256]{1,0:T(8,128)(2,1)} %get-tuple-element.10) | copy-start | bytes 811012
  7.7 7.9 %copy-start.1 = (bf16[1056,256]{1,0:T(8,128)(2,1)S(1)}, bf16[1056,256]{1,0:T(8,128)(2,1)}, u32[]{:S(2)}) copy-start(bf16[1056,256]{1,0:T(8,128)(2,1)} %get-tuple-element.9.after_ref) | copy-start | bytes 1622020
  7.7 74.7 %all-to-all-start = ((bf16[16,2,64,512]{3,2,1,0:T(8,128)(2,1)}), bf16[16,2,64,512]{3,2,1,0:T(8,128)(2,1)S(1)}, u32[]{:S(2)}, u32[]{:S(2)}) async-start(bf16[16,2,64,512]{3,2,1,0:T(8,128)(2,1)} %query_projection.1), calls=%async_computation | async-start | bytes 4194304 | tf_op jit(solution)/shard_map/all_to_all | solution.py:314
  13.8 1.8 %collective-permute-start = (bf16[528,256]{1,0:T(8,128)(2,1)S(1)}, bf16[528,256]{1,0:T(8,128)(2,1)S(1)}, u32[]{:S(2)}, u32[]{:S(2)}) collective-permute-start(bf16[528,256]{1,0:T(8,128)(2,1)S(1)} %copy-done.7), channel_id=1, source_target_pairs={{0,1},{1,0},{2,3},{3,2},{4,5},{5,4},{6,7},{7,6},{8,9},{9,8},{10,11... | collective-permute-start | bytes 811016 | tf_op jit(solution)/shard_map/ppermute | solution.py:295
  15.6 66.7 %copy-start.2 = (bf16[1056,256]{1,0:T(8,128)(2,1)}, bf16[1056,256]{1,0:T(8,128)(2,1)S(1)}, u32[]{:S(2)}) copy-start(bf16[1056,256]{1,0:T(8,128)(2,1)S(1)} %constant_dynamic-update-slice_fusion.refs_0_) | copy-start | bytes 1622020
  15.7 34.7 %collective-permute-start.3 = (bf16[1056,256]{1,0:T(8,128)(2,1)S(1)}, bf16[1056,256]{1,0:T(8,128)(2,1)S(1)}, u32[]{:S(2)}, u32[]{:S(2)}) collective-permute-start(bf16[1056,256]{1,0:T(8,128)(2,1)S(1)} %constant_dynamic-update-slice_fusion.refs_0_), channel_id=1, source_target_pairs={{0,8},{1,9},{2,10},{3,11},{4,12},{5,13},{6,14},{7,15},{8,0},{9,1},... | collective-permute-start | bytes 1622024 | tf_op jit(solution)/shard_map/ppermute | solution.py:294
  16.0 34.6 %collective-permute-start.2 = (bf16[1056,256]{1,0:T(8,128)(2,1)S(1)}, bf16[1056,256]{1,0:T(8,128)(2,1)}, u32[]{:S(2)}, u32[]{:S(2)}) collective-permute-start(bf16[1056,256]{1,0:T(8,128)(2,1)S(1)} %constant_dynamic-update-slice_fusion.refs_0_), channel_id=1, source_target_pairs={{0,6},{1,7},{2,0},{3,1},{4,2},{5,3},{6,4},{7,5},{8,14},{9,15},{10,... | collective-permute-start | bytes 1622024 | tf_op jit(solution)/shard_map/ppermute | solution.py:293
  50.3 3.0 %copy-start.5 = (bf16[1056,256]{1,0:T(8,128)(2,1)}, bf16[1056,256]{1,0:T(8,128)(2,1)S(1)}, u32[]{:S(2)}) copy-start(bf16[1056,256]{1,0:T(8,128)(2,1)S(1)} %collective-permute-done.3.refs_3_) | copy-start | bytes 1622020
  50.3 14.7 %collective-permute-start.4 = (bf16[1056,256]{1,0:T(8,128)(2,1)S(1)}, bf16[1056,256]{1,0:T(8,128)(2,1)S(1)}, u32[]{:S(2)}, u32[]{:S(2)}) collective-permute-start(bf16[1056,256]{1,0:T(8,128)(2,1)S(1)} %collective-permute-done.3.refs_3_), channel_id=1, source_target_pairs={{0,2},{1,3},{2,4},{3,5},{4,6},{5,7},{6,0},{7,1},{8,10},{9,11},{10,... | collective-permute-start | bytes 1622024 | tf_op jit(solution)/shard_map/ppermute | solution.py:292
  50.6 15.2 %collective-permute-start.5 = (bf16[1056,256]{1,0:T(8,128)(2,1)}, bf16[1056,256]{1,0:T(8,128)(2,1)S(1)}, u32[]{:S(2)}, u32[]{:S(2)}) collective-permute-start(bf16[1056,256]{1,0:T(8,128)(2,1)} %collective-permute-done.2.refs_2_), channel_id=1, source_target_pairs={{0,6},{1,7},{2,0},{3,1},{4,2},{5,3},{6,4},{7,5},{8,14},{9,15},{10,... | collective-permute-start | bytes 1622024 | tf_op jit(solution)/shard_map/ppermute | solution.py:293
  53.4 23.3 %collective-permute-start.1 = (bf16[1056,256]{1,0:T(8,128)(2,1)S(1)}, bf16[1056,256]{1,0:T(8,128)(2,1)}, u32[]{:S(2)}, u32[]{:S(2)}) collective-permute-start(bf16[1056,256]{1,0:T(8,128)(2,1)S(1)} %constant_dynamic-update-slice_fusion.refs_0_), channel_id=1, source_target_pairs={{0,2},{1,3},{2,4},{3,5},{4,6},{5,7},{6,0},{7,1},{8,10},{9,11},{10,... | collective-permute-start | bytes 1622024 | tf_op jit(solution)/shard_map/ppermute | solution.py:292
  53.4 23.3 %collective-permute-start.6 = (bf16[1056,256]{1,0:T(8,128)(2,1)}, bf16[1056,256]{1,0:T(8,128)(2,1)}, u32[]{:S(2)}, u32[]{:S(2)}) collective-permute-start(bf16[1056,256]{1,0:T(8,128)(2,1)} %collective-permute-done.2.refs_2_), channel_id=1, source_target_pairs={{0,8},{1,9},{2,10},{3,11},{4,12},{5,13},{6,14},{7,15},{8,0},{9,1},... | collective-permute-start | bytes 1622024 | tf_op jit(solution)/shard_map/ppermute | solution.py:294
  65.1 17.3 %copy-start.3 = (bf16[1056,256]{1,0:T(8,128)(2,1)}, bf16[1056,256]{1,0:T(8,128)(2,1)S(1)}, u32[]{:S(2)}) copy-start(bf16[1056,256]{1,0:T(8,128)(2,1)S(1)} %collective-permute-done.4.refs_4_) | copy-start | bytes 1622020
  65.8 16.5 %collective-permute-start.7 = (bf16[528,256]{1,0:T(8,128)(2,1)}, bf16[528,256]{1,0:T(8,128)(2,1)S(1)}, u32[]{:S(2)}, u32[]{:S(2)}) collective-permute-start(bf16[528,256]{1,0:T(8,128)(2,1)} %slice.8), channel_id=1, source_target_pairs={{0,2},{1,3},{2,4},{3,5},{4,6},{5,7},{6,0},{7,1},{8,10},{9,11},{10,... | collective-permute-start | bytes 811016 | tf_op jit(solution)/shard_map/ppermute | solution.py:292
  65.8 0.8 copy-start.4
  67.4 15.0 %collective-permute-start.8 = (bf16[528,256]{1,0:T(8,128)(2,1)}, bf16[528,256]{1,0:T(8,128)(2,1)}, u32[]{:S(2)}, u32[]{:S(2)}) collective-permute-start(bf16[528,256]{1,0:T(8,128)(2,1)} %slice.9), channel_id=1, source_target_pairs={{0,8},{1,9},{2,10},{3,11},{4,12},{5,13},{6,14},{7,15},{8,0},{9,1},... | collective-permute-start | bytes 811016 | tf_op jit(solution)/shard_map/ppermute | solution.py:294
  82.3 0.7 copy-start.6
  83.1 1.3 copy-start
  143.1 3.4 %collective-permute-start.9 = (bf16[512,512]{1,0:T(8,128)(2,1)}, bf16[512,512]{1,0:T(8,128)(2,1)S(1)}, u32[]{:S(2)}, u32[]{:S(2)}) collective-permute-start(bf16[512,512]{1,0:T(8,128)(2,1)} %get-tuple-element.12), channel_id=1, source_target_pairs={{0,1},{1,0},{2,3},{3,2},{4,5},{5,4},{6,7},{7,6},{8,9},{9,8},{10,11... | collective-permute-start | bytes 1572872 | tf_op jit(solution)/shard_map/ppermute | solution.py:295

commit v3 on v2

--- a/solution.py
+++ b/solution.py
@@ -171,7 +171,8 @@
 
     chip_rows = 2 * per_dev
     first = my_chip * chip_rows
-    anchor = start_of(first) // BLK * BLK
+    low_first = start_of(first)
+    anchor = low_first // TK * TK
 
     for copy in q_copies:
         copy.wait()
@@ -194,9 +195,8 @@
 
     lax.fori_loop(0, (first + chip_rows - anchor + TK - 1) // TK, turn, 0)
 
-    low_last = start_of(first + chip_rows - 1)
-
-    def attend(work, k, v, allowed):
+
+    def attend(work, k, v, allowed=None, columns=None):
         def score(u):
             s = jnp.dot(k, q_t[u], preferred_element_type=jnp.float32)
             return s if allowed is None else jnp.where(allowed, s, NEGATIVE_FILL)
@@ -206,7 +206,11 @@
             following = score(work[n + 1]) if n + 1 < len(work) else None
             m_old = m_ref[u]
             m_new = jnp.maximum(m_old, jnp.max(s, axis=0, keepdims=True))
-            p = jnp.exp2(s - m_new)
+            shift = m_new
+            if columns is not None:
+                shift = jnp.where(columns[units[u][0]], m_new, -NEGATIVE_FILL)
+                m_new = jnp.where(columns[units[u][0]], m_new, m_old)
+            p = jnp.exp2(s - shift)
             shrink = jnp.exp2(m_old - m_new)
             m_ref[u] = m_new
             l_ref[u] = l_ref[u] * shrink + jnp.sum(p, axis=0, keepdims=True)
@@ -221,11 +225,15 @@
 
     def step(t, carry):
         k0 = pl.multiple_of(anchor + t * TK, BLK)
-        clear = (k0 >= low_last) & (k0 + TK - 1 <= first)
+        clear = (k0 >= low_first) & (k0 + TK <= first)
 
         @pl.when(clear)
         def _():
-            attend(range(len(units)), keys_at(k0, TK), v_t[t], None)
+            columns = []
+            for tq in range(chip_rows // TQ):
+                qpos = first + tq * TQ + lax.broadcasted_iota(jnp.int32, (1, TQ), 1)
+                columns.append(start_of(qpos) <= k0)
+            attend(range(len(units)), keys_at(k0, TK), v_t[t], columns=columns)
 
         for tq in range(chip_rows // TQ):
             for piece in range(TK // TQ):
@@ -242,7 +250,7 @@
                         [tq * GROUP + h for h in range(GROUP)],
                         keys_at(from_key, TQ),
                         v_t[t, :, piece * TQ : (piece + 1) * TQ],
-                        allowed,
+                        allowed=allowed,
                     )
 
         return carry
@@ -302,6 +310,7 @@
         name="kv_projection",
     )(core[None], destination, segment, events, key_weight, value_weight)
     theirs = swap(other)
+    mine = lax.dynamic_update_slice(own, theirs, (rows + META, 0))
     q_send = pl.pallas_call(
         q_kernel,
         out_shape=jax.ShapeDtypeStruct((ndev, 2, BLK, half), jnp.bfloat16),
@@ -309,8 +318,7 @@
         out_specs=hbm,
         scratch_shapes=[VMEM((2, rows, half), jnp.bfloat16), pltpu.SemaphoreType.DMA((rows // BLK * 2,))],
         name="query_projection",
-    )(destination, events, w_query, own)
-    mine = lax.dynamic_update_slice(own, theirs, (rows + META, 0))
+    )(destination, events, w_query, mine)
     q_got = lax.all_to_all(q_send, "ctx", split_axis=0, concat_axis=0, tiled=True)
     shard_rows = rows + META
     y_down = up(mine)

time: 148 us -> 136 us (0.919)
  the two profiles are of different devices: /device:TPU:51 before, /device:TPU:19 now
where the time goes in v3:
time: 136 us; the launch traced here: 135 us
  waiting for transfers between devices  63.6 us (47%)
  Pallas kernels  51.8 us (38%)
  starting transfers between devices  13.4 us (10%)
  local copies, waits for them, and re-layouts  5.89 us (4%)
    pallas_call x1, Pallas kernels, on_device(): pl.pallas_call(attention_kernel, out_shape=(jax.ShapeDtypeStruct((rows, w...  44.2 us
    ppermute x3, waiting for transfers between devices, on_device(): across = lambda a: lax.ppermute(a, 'ctx', pairs(1, 0, 0))  35.9 us
    ppermute x3, waiting for transfers between devices, on_device(): up = lambda a: lax.ppermute(a, 'ctx', pairs(0, 1, 0))  24.6 us
    all_to_all x1, starting transfers between devices, on_device(): lax.all_to_all(q_send, 'ctx', split_axis=0, concat_axis=0, tiled=True)  5.9 us
    pallas_call x1, Pallas kernels, on_device(): pl.pallas_call(q_kernel, out_shape=jax.ShapeDtypeStruct((ndev, 2, BLK, ha...  4.28 us
    pallas_call x1, Pallas kernels, on_device(): pl.pallas_call(kv_kernel, out_shape=(jax.ShapeDtypeStruct((2 * (rows + ME...  3.32 us
    ppermute x2, waiting for transfers between devices, on_device(): swap = lambda a: lax.ppermute(a, 'ctx', pairs(0, 0, 1))  3.13 us
    ppermute x2, starting transfers between devices, on_device(): down = lambda a: lax.ppermute(a, 'ctx', pairs(0, -1, 0))  3.06 us
  transfers between devices with their start and end apart: 11, of which 6 were waited for; matrix products, arithmetic and copies ran while one was open for 2% of the time, Pallas kernels for 0%

profile of v3, /device:TPU:19, one launch (start us, length us, event | category | flops | bytes accessed | tf_op | source)
XLA Modules:
  0.0 135.3 jit_solution(1983476616088551762)
XLA Ops:
  0.0 3.3 %kv_projection.1 = (bf16[1056,256]{1,0:T(8,128)(2,1)}, bf16[528,256]{1,0:T(8,128)(2,1)}) custom-call(s32[1]{0:T(128)} %bitcast.2.core_ref, s32[512]{0:T(512)} %dest_ref.3, s32[512]{0:T(512)} %seg_ref.1, bf16[512,1024]{1,0:T(8,128)(2,1)} %ev_ref.3, bf16[1024,256]{1,0:T(8,128)(2,1)} %kw_ref.1, bf16[1024,256]{1,0:T(8,128)(2,1)} %vw_ref.1), custom_call_target="tpu_custom_call" | custom-call | tf_op jit(solution)/shard_map/kv_projection/pallas_call | solution.py:305
  3.3 0.7 collective-permute-start
  4.0 1.4 %collective-permute-done = bf16[528,256]{1,0:T(8,128)(2,1)S(1)} collective-permute-done((bf16[528,256]{1,0:T(8,128)(2,1)}, bf16[528,256]{1,0:T(8,128)(2,1)S(1)}, u32[]{:S(2)}, u32[]{:S(2)}) %collective-permute-start) | collective-permute-done | bytes 270368 | tf_op jit(solution)/shard_map/ppermute | solution.py:303
  5.4 0.7 constant_dynamic-update-slice_fusion.after_ref.refs_0_
  6.1 4.3 %query_projection.1 = bf16[16,2,64,512]{3,2,1,0:T(8,128)(2,1)} custom-call(s32[512]{0:T(512)} %dest_ref.3, bf16[512,1024]{1,0:T(8,128)(2,1)} %ev_ref.3, bf16[1024,1024]{1,0:T(8,128)(2,1)} %wq_ref.1, bf16[1056,256]{1,0:T(8,128)(2,1)} %constant_dynamic-update-slice_fusion.after_ref.refs_0_), custom_call_target="tpu_custom_call" | custom-call | tf_op jit(solution)/shard_map/query_projection/pallas_call | solution.py:314
  10.4 5.9 %all-to-all-start = ((bf16[16,2,64,512]{3,2,1,0:T(8,128)(2,1)}), bf16[16,2,64,512]{3,2,1,0:T(8,128)(2,1)S(1)}, u32[]{:S(2)}, u32[]{:S(2)}) async-start(bf16[16,2,64,512]{3,2,1,0:T(8,128)(2,1)} %query_projection.1), calls=%async_computation | async-start | bytes 4194304 | tf_op jit(solution)/shard_map/all_to_all | solution.py:322
  16.3 0.4 collective-permute-start.3
  16.7 0.3 collective-permute-start.2
  17.0 35.9 %collective-permute-done.3.refs_3_ = bf16[1056,256]{1,0:T(8,128)(2,1)S(1)} collective-permute-done((bf16[1056,256]{1,0:T(8,128)(2,1)S(1)}, bf16[1056,256]{1,0:T(8,128)(2,1)S(1)}, u32[]{:S(2)}, u32[]{:S(2)}) %collective-permute-start.3) | collective-permute-done | bytes 540704 | tf_op jit(solution)/shard_map/ppermute | solution.py:302
  52.9 0.2 collective-permute-start.4
  53.1 0.0 collective-permute-done.2.refs_2_
  53.1 2.8 %collective-permute-start.5 = (bf16[1056,256]{1,0:T(8,128)(2,1)}, bf16[1056,256]{1,0:T(8,128)(2,1)S(1)}, u32[]{:S(2)}, u32[]{:S(2)}) collective-permute-start(bf16[1056,256]{1,0:T(8,128)(2,1)} %collective-permute-done.2.refs_2_), channel_id=1, source_target_pairs={{0,6},{1,7},{2,0},{3,1},{4,2},{5,3},{6,4},{7,5},{8,14},{9,15},{10,... | collective-permute-start | bytes 1622024 | tf_op jit(solution)/shard_map/ppermute | solution.py:301
  55.9 0.0 collective-permute-start.1
  55.9 0.8 collective-permute-start.6
  56.6 10.9 %collective-permute-done.4.refs_4_ = bf16[1056,256]{1,0:T(8,128)(2,1)S(1)} collective-permute-done((bf16[1056,256]{1,0:T(8,128)(2,1)S(1)}, bf16[1056,256]{1,0:T(8,128)(2,1)S(1)}, u32[]{:S(2)}, u32[]{:S(2)}) %collective-permute-start.4) | collective-permute-done | bytes 540704 | tf_op jit(solution)/shard_map/ppermute | solution.py:300
  67.6 0.8 slice.8
  68.3 0.0 collective-permute-start.7
  68.4 0.0 collective-permute-done.5.refs_5_
  68.4 0.8 copy-done.3
  69.2 0.7 slice.9
  69.9 0.8 collective-permute-start.8
  70.6 0.6 pad_add_fusion.where_ref
  71.2 7.9 %collective-permute-done.1.refs_1_ = bf16[1056,256]{1,0:T(8,128)(2,1)} collective-permute-done((bf16[1056,256]{1,0:T(8,128)(2,1)S(1)}, bf16[1056,256]{1,0:T(8,128)(2,1)}, u32[]{:S(2)}, u32[]{:S(2)}) %collective-permute-start.1) | collective-permute-done | bytes 540704 | tf_op jit(solution)/shard_map/ppermute | solution.py:300
  79.2 0.0 collective-permute-done.6.refs_6_
  79.2 5.7 %collective-permute-done.7.refs_7_ = bf16[528,256]{1,0:T(8,128)(2,1)S(1)} collective-permute-done((bf16[528,256]{1,0:T(8,128)(2,1)}, bf16[528,256]{1,0:T(8,128)(2,1)S(1)}, u32[]{:S(2)}, u32[]{:S(2)}) %collective-permute-start.7) | collective-permute-done | bytes 270368 | tf_op jit(solution)/shard_map/ppermute | solution.py:300
  84.9 0.0 collective-permute-done.8.refs_8_
  84.9 0.7 copy-done.5
  85.6 1.3 copy-done
  86.9 44.2 %attention.1 = (bf16[512,1024]{1,0:T(8,128)(2,1)}, bf16[512,512]{1,0:T(8,128)(2,1)}) custom-call(s32[3]{0:T(128)} %pad_add_fusion.where_ref, bf16[1056,256]{1,0:T(8,128)(2,1)} %constant_dynamic-update-slice_fusion.after_ref.refs_0_, bf16[1056,256]{1,0:T(8,128)(2,1)} %collective-permute-done.1.refs_1_, bf16[1056,256]{1,0:T(8,128)(2,1)} %collective-permute-done.2.refs_2_, ...), custom_call_target="tpu_custom_call" | custom-call | tf_op jit(solution)/shard_map/attention/pallas_call | solution.py:334
  131.1 1.6 %collective-permute-start.9 = (bf16[512,512]{1,0:T(8,128)(2,1)}, bf16[512,512]{1,0:T(8,128)(2,1)S(1)}, u32[]{:S(2)}, u32[]{:S(2)}) collective-permute-start(bf16[512,512]{1,0:T(8,128)(2,1)} %get-tuple-element.12), channel_id=1, source_target_pairs={{0,1},{1,0},{2,3},{3,2},{4,5},{5,4},{6,7},{7,6},{8,9},{9,8},{10,11... | collective-permute-start | bytes 1572872 | tf_op jit(solution)/shard_map/ppermute | solution.py:303
  132.8 1.7 %collective-permute-done.9 = bf16[512,512]{1,0:T(8,128)(2,1)S(1)} collective-permute-done((bf16[512,512]{1,0:T(8,128)(2,1)}, bf16[512,512]{1,0:T(8,128)(2,1)S(1)}, u32[]{:S(2)}, u32[]{:S(2)}) %collective-permute-start.9) | collective-permute-done | bytes 524320 | tf_op jit(solution)/shard_map/ppermute | solution.py:303
  134.5 0.8 constant_dynamic-update-slice_fusion.1
  (10 shorter events, 0.0 us)
Async XLA Ops:
  3.3 2.1 %collective-permute-start = (bf16[528,256]{1,0:T(8,128)(2,1)}, bf16[528,256]{1,0:T(8,128)(2,1)S(1)}, u32[]{:S(2)}, u32[]{:S(2)}) collective-permute-start(bf16[528,256]{1,0:T(8,128)(2,1)} %get-tuple-element.10), channel_id=1, source_target_pairs={{0,1},{1,0},{2,3},{3,2},{4,5},{5,4},{6,7},{7,6},{8,9},{9,8},{10,11... | collective-permute-start | bytes 811016 | tf_op jit(solution)/shard_map/ppermute | solution.py:303
  10.4 5.9 %copy-start.1 = (bf16[1056,256]{1,0:T(8,128)(2,1)S(1)}, bf16[1056,256]{1,0:T(8,128)(2,1)}, u32[]{:S(2)}) copy-start(bf16[1056,256]{1,0:T(8,128)(2,1)} %constant_dynamic-update-slice_fusion.after_ref.refs_0_) | copy-start | bytes 1622020
  10.4 74.4 %all-to-all-start = ((bf16[16,2,64,512]{3,2,1,0:T(8,128)(2,1)}), bf16[16,2,64,512]{3,2,1,0:T(8,128)(2,1)S(1)}, u32[]{:S(2)}, u32[]{:S(2)}) async-start(bf16[16,2,64,512]{3,2,1,0:T(8,128)(2,1)} %query_projection.1), calls=%async_computation | async-start | bytes 4194304 | tf_op jit(solution)/shard_map/all_to_all | solution.py:322
  16.3 36.5 %collective-permute-start.3 = (bf16[1056,256]{1,0:T(8,128)(2,1)S(1)}, bf16[1056,256]{1,0:T(8,128)(2,1)S(1)}, u32[]{:S(2)}, u32[]{:S(2)}) collective-permute-start(bf16[1056,256]{1,0:T(8,128)(2,1)S(1)} %copy-done.1), channel_id=1, source_target_pairs={{0,8},{1,9},{2,10},{3,11},{4,12},{5,13},{6,14},{7,15},{8,0},{9,1},... | collective-permute-start | bytes 1622024 | tf_op jit(solution)/shard_map/ppermute | solution.py:302
  16.7 36.4 %collective-permute-start.2 = (bf16[1056,256]{1,0:T(8,128)(2,1)S(1)}, bf16[1056,256]{1,0:T(8,128)(2,1)}, u32[]{:S(2)}, u32[]{:S(2)}) collective-permute-start(bf16[1056,256]{1,0:T(8,128)(2,1)S(1)} %copy-done.1), channel_id=1, source_target_pairs={{0,6},{1,7},{2,0},{3,1},{4,2},{5,3},{6,4},{7,5},{8,14},{9,15},{10,... | collective-permute-start | bytes 1622024 | tf_op jit(solution)/shard_map/ppermute | solution.py:301
  52.9 3.0 %copy-start.4 = (bf16[1056,256]{1,0:T(8,128)(2,1)}, bf16[1056,256]{1,0:T(8,128)(2,1)S(1)}, u32[]{:S(2)}) copy-start(bf16[1056,256]{1,0:T(8,128)(2,1)S(1)} %collective-permute-done.3.refs_3_) | copy-start | bytes 1622020
  52.9 14.7 %collective-permute-start.4 = (bf16[1056,256]{1,0:T(8,128)(2,1)S(1)}, bf16[1056,256]{1,0:T(8,128)(2,1)S(1)}, u32[]{:S(2)}, u32[]{:S(2)}) collective-permute-start(bf16[1056,256]{1,0:T(8,128)(2,1)S(1)} %collective-permute-done.3.refs_3_), channel_id=1, source_target_pairs={{0,2},{1,3},{2,4},{3,5},{4,6},{5,7},{6,0},{7,1},{8,10},{9,11},{10,... | collective-permute-start | bytes 1622024 | tf_op jit(solution)/shard_map/ppermute | solution.py:300
  53.1 15.3 %collective-permute-start.5 = (bf16[1056,256]{1,0:T(8,128)(2,1)}, bf16[1056,256]{1,0:T(8,128)(2,1)S(1)}, u32[]{:S(2)}, u32[]{:S(2)}) collective-permute-start(bf16[1056,256]{1,0:T(8,128)(2,1)} %collective-permute-done.2.refs_2_), channel_id=1, source_target_pairs={{0,6},{1,7},{2,0},{3,1},{4,2},{5,3},{6,4},{7,5},{8,14},{9,15},{10,... | collective-permute-start | bytes 1622024 | tf_op jit(solution)/shard_map/ppermute | solution.py:301
  55.9 23.3 %collective-permute-start.1 = (bf16[1056,256]{1,0:T(8,128)(2,1)S(1)}, bf16[1056,256]{1,0:T(8,128)(2,1)}, u32[]{:S(2)}, u32[]{:S(2)}) collective-permute-start(bf16[1056,256]{1,0:T(8,128)(2,1)S(1)} %copy-done.1), channel_id=1, source_target_pairs={{0,2},{1,3},{2,4},{3,5},{4,6},{5,7},{6,0},{7,1},{8,10},{9,11},{10,... | collective-permute-start | bytes 1622024 | tf_op jit(solution)/shard_map/ppermute | solution.py:300
  55.9 23.3 %collective-permute-start.6 = (bf16[1056,256]{1,0:T(8,128)(2,1)}, bf16[1056,256]{1,0:T(8,128)(2,1)}, u32[]{:S(2)}, u32[]{:S(2)}) collective-permute-start(bf16[1056,256]{1,0:T(8,128)(2,1)} %collective-permute-done.2.refs_2_), channel_id=1, source_target_pairs={{0,8},{1,9},{2,10},{3,11},{4,12},{5,13},{6,14},{7,15},{8,0},{9,1},... | collective-permute-start | bytes 1622024 | tf_op jit(solution)/shard_map/ppermute | solution.py:302
  67.6 17.3 %copy-start.2 = (bf16[1056,256]{1,0:T(8,128)(2,1)}, bf16[1056,256]{1,0:T(8,128)(2,1)S(1)}, u32[]{:S(2)}) copy-start(bf16[1056,256]{1,0:T(8,128)(2,1)S(1)} %collective-permute-done.4.refs_4_) | copy-start | bytes 1622020
  68.3 16.5 %collective-permute-start.7 = (bf16[528,256]{1,0:T(8,128)(2,1)}, bf16[528,256]{1,0:T(8,128)(2,1)S(1)}, u32[]{:S(2)}, u32[]{:S(2)}) collective-permute-start(bf16[528,256]{1,0:T(8,128)(2,1)} %slice.8), channel_id=1, source_target_pairs={{0,2},{1,3},{2,4},{3,5},{4,6},{5,7},{6,0},{7,1},{8,10},{9,11},{10,... | collective-permute-start | bytes 811016 | tf_op jit(solution)/shard_map/ppermute | solution.py:300
  68.4 0.8 copy-start.3
  69.9 15.0 %collective-permute-start.8 = (bf16[528,256]{1,0:T(8,128)(2,1)}, bf16[528,256]{1,0:T(8,128)(2,1)}, u32[]{:S(2)}, u32[]{:S(2)}) collective-permute-start(bf16[528,256]{1,0:T(8,128)(2,1)} %slice.9), channel_id=1, source_target_pairs={{0,8},{1,9},{2,10},{3,11},{4,12},{5,13},{6,14},{7,15},{8,0},{9,1},... | collective-permute-start | bytes 811016 | tf_op jit(solution)/shard_map/ppermute | solution.py:302
  84.9 0.7 copy-start.5
  85.6 1.3 copy-start
  131.1 3.4 %collective-permute-start.9 = (bf16[512,512]{1,0:T(8,128)(2,1)}, bf16[512,512]{1,0:T(8,128)(2,1)S(1)}, u32[]{:S(2)}, u32[]{:S(2)}) collective-permute-start(bf16[512,512]{1,0:T(8,128)(2,1)} %get-tuple-element.12), channel_id=1, source_target_pairs={{0,1},{1,0},{2,3},{3,2},{4,5},{5,4},{6,7},{7,6},{8,9},{9,8},{10,11... | collective-permute-start | bytes 1572872 | tf_op jit(solution)/shard_map/ppermute | solution.py:303

commit v4 on v3

--- a/solution.py
+++ b/solution.py
@@ -199,7 +199,7 @@
     def attend(work, k, v, allowed=None, columns=None):
         def score(u):
             s = jnp.dot(k, q_t[u], preferred_element_type=jnp.float32)
-            return s if allowed is None else jnp.where(allowed, s, NEGATIVE_FILL)
+            return s if allowed is None else jnp.where(allowed[units[u][0]], s, NEGATIVE_FILL)
 
         s = score(work[0])
         for n, u in enumerate(work):
@@ -235,23 +235,33 @@
                 columns.append(start_of(qpos) <= k0)
             attend(range(len(units)), keys_at(k0, TK), v_t[t], columns=columns)
 
-        for tq in range(chip_rows // TQ):
-            for piece in range(TK // TQ):
+        for piece in range(TK // TQ):
+            from_key = pl.multiple_of(k0 + piece * TQ, BLK)
+
+            def masked(tiles, piece=piece, from_key=from_key):
+                kpos = from_key + lax.broadcasted_iota(jnp.int32, (TQ, TQ), 0)
+                allowed = {}
+                for tq in tiles:
+                    qpos = first + tq * TQ + lax.broadcasted_iota(jnp.int32, (1, TQ), 1)
+                    allowed[tq] = (kpos <= qpos) & (kpos >= start_of(qpos))
+                attend(
+                    [u for u, (tq, _) in enumerate(units) if tq in tiles],
+                    keys_at(from_key, TQ),
+                    v_t[t, :, piece * TQ : (piece + 1) * TQ],
+                    allowed=allowed,
+                )
+
+            def used(tq, from_key=from_key):
                 p0 = first + tq * TQ
-                from_key = pl.multiple_of(k0 + piece * TQ, BLK)
-                used = (from_key <= p0 + TQ - 1) & (from_key + TQ - 1 >= start_of(p0))
-
-                @pl.when(jnp.logical_not(clear) & used)
-                def _(tq=tq, piece=piece, p0=p0, from_key=from_key):
-                    kpos = from_key + lax.broadcasted_iota(jnp.int32, (TQ, TQ), 0)
-                    qpos = p0 + lax.broadcasted_iota(jnp.int32, (1, TQ), 1)
-                    allowed = (kpos <= qpos) & (kpos >= start_of(qpos))
-                    attend(
-                        [tq * GROUP + h for h in range(GROUP)],
-                        keys_at(from_key, TQ),
-                        v_t[t, :, piece * TQ : (piece + 1) * TQ],
-                        allowed=allowed,
-                    )
+                return (from_key <= p0 + TQ - 1) & (from_key + TQ - 1 >= start_of(p0))
+
+            @pl.when(jnp.logical_not(clear) & used(0))
+            def _(masked=masked):
+                masked((0, 1))
+
+            @pl.when(jnp.logical_not(clear) & jnp.logical_not(used(0)) & used(1))
+            def _(masked=masked):
+                masked((1,))
 
         return carry
 

time: 136 us -> 137 us (level)
  the two profiles are of different devices: /device:TPU:19 before, /device:TPU:123 now
where the time goes in v4:
time: 137 us
  waiting for transfers between devices  56.7 us (41%)
  Pallas kernels  55.8 us (41%)
  starting transfers between devices  18 us (13%)
  local copies, waits for them, and re-layouts  5.89 us (4%)
    pallas_call x1, Pallas kernels, on_device(): pl.pallas_call(attention_kernel, out_shape=(jax.ShapeDtypeStruct((rows, w...  48.2 us
    ppermute x3, waiting for transfers between devices, on_device(): across = lambda a: lax.ppermute(a, 'ctx', pairs(1, 0, 0))  35 us
    ppermute x3, waiting for transfers between devices, on_device(): up = lambda a: lax.ppermute(a, 'ctx', pairs(0, 1, 0))  18.6 us
    ppermute x3, starting transfers between devices, on_device(): up = lambda a: lax.ppermute(a, 'ctx', pairs(0, 1, 0))  7.37 us
    all_to_all x1, starting transfers between devices, on_device(): lax.all_to_all(q_send, 'ctx', split_axis=0, concat_axis=0, tiled=True)  5.74 us
    pallas_call x1, Pallas kernels, on_device(): pl.pallas_call(q_kernel, out_shape=jax.ShapeDtypeStruct((ndev, 2, BLK, ha...  4.3 us
    pallas_call x1, Pallas kernels, on_device(): pl.pallas_call(kv_kernel, out_shape=(jax.ShapeDtypeStruct((2 * (rows + ME...  3.32 us
    ppermute x2, waiting for transfers between devices, on_device(): swap = lambda a: lax.ppermute(a, 'ctx', pairs(0, 0, 1))  3.13 us
  transfers between devices with their start and end apart: 11, of which 6 were waited for; matrix products, arithmetic and copies ran while one was open for 2% of the time, Pallas kernels for 0%

profile of v4, /device:TPU:123, one launch (start us, length us, event | category | flops | bytes accessed | tf_op | source)
XLA Modules:
  0.0 137.1 jit_solution(16494278569803423199)
XLA Ops:
  0.0 3.3 %kv_projection.1 = (bf16[1056,256]{1,0:T(8,128)(2,1)}, bf16[528,256]{1,0:T(8,128)(2,1)}) custom-call(s32[1]{0:T(128)} %bitcast.2.core_ref, s32[512]{0:T(512)} %dest_ref.3, s32[512]{0:T(512)} %seg_ref.1, bf16[512,1024]{1,0:T(8,128)(2,1)} %ev_ref.3, bf16[1024,256]{1,0:T(8,128)(2,1)} %kw_ref.1, bf16[1024,256]{1,0:T(8,128)(2,1)} %vw_ref.1), custom_call_target="tpu_custom_call" | custom-call | tf_op jit(solution)/shard_map/kv_projection/pallas_call | solution.py:315
  3.3 0.7 collective-permute-start
  4.0 1.4 %collective-permute-done = bf16[528,256]{1,0:T(8,128)(2,1)S(1)} collective-permute-done((bf16[528,256]{1,0:T(8,128)(2,1)}, bf16[528,256]{1,0:T(8,128)(2,1)S(1)}, u32[]{:S(2)}, u32[]{:S(2)}) %collective-permute-start) | collective-permute-done | bytes 270368 | tf_op jit(solution)/shard_map/ppermute | solution.py:313
  5.4 0.7 constant_dynamic-update-slice_fusion.after_ref.refs_0_
  6.1 4.3 %query_projection.1 = bf16[16,2,64,512]{3,2,1,0:T(8,128)(2,1)} custom-call(s32[512]{0:T(512)} %dest_ref.3, bf16[512,1024]{1,0:T(8,128)(2,1)} %ev_ref.3, bf16[1024,1024]{1,0:T(8,128)(2,1)} %wq_ref.1, bf16[1056,256]{1,0:T(8,128)(2,1)} %constant_dynamic-update-slice_fusion.after_ref.refs_0_), custom_call_target="tpu_custom_call" | custom-call | tf_op jit(solution)/shard_map/query_projection/pallas_call | solution.py:324
  10.4 5.7 %all-to-all-start = ((bf16[16,2,64,512]{3,2,1,0:T(8,128)(2,1)}), bf16[16,2,64,512]{3,2,1,0:T(8,128)(2,1)S(1)}, u32[]{:S(2)}, u32[]{:S(2)}) async-start(bf16[16,2,64,512]{3,2,1,0:T(8,128)(2,1)} %query_projection.1), calls=%async_computation | async-start | bytes 4194304 | tf_op jit(solution)/shard_map/all_to_all | solution.py:332
  16.2 0.4 collective-permute-start.3
  16.5 0.6 collective-permute-start.2
  17.1 34.9 %collective-permute-done.3.refs_3_ = bf16[1056,256]{1,0:T(8,128)(2,1)S(1)} collective-permute-done((bf16[1056,256]{1,0:T(8,128)(2,1)S(1)}, bf16[1056,256]{1,0:T(8,128)(2,1)S(1)}, u32[]{:S(2)}, u32[]{:S(2)}) %collective-permute-start.3) | collective-permute-done | bytes 540704 | tf_op jit(solution)/shard_map/ppermute | solution.py:312
  52.1 1.3 collective-permute-start.4
  53.3 0.0 collective-permute-done.2.refs_2_
  53.3 0.2 collective-permute-start.5
  53.5 3.3 %collective-permute-start.1 = (bf16[1056,256]{1,0:T(8,128)(2,1)S(1)}, bf16[1056,256]{1,0:T(8,128)(2,1)}, u32[]{:S(2)}, u32[]{:S(2)}) collective-permute-start(bf16[1056,256]{1,0:T(8,128)(2,1)S(1)} %copy-done.1), channel_id=1, source_target_pairs={{0,2},{1,3},{2,4},{3,5},{4,6},{5,7},{6,0},{7,1},{8,10},{9,11},{10,... | collective-permute-start | bytes 1622024 | tf_op jit(solution)/shard_map/ppermute | solution.py:310
  56.8 0.8 collective-permute-start.6
  57.6 7.5 %collective-permute-done.4.refs_4_ = bf16[1056,256]{1,0:T(8,128)(2,1)S(1)} collective-permute-done((bf16[1056,256]{1,0:T(8,128)(2,1)S(1)}, bf16[1056,256]{1,0:T(8,128)(2,1)S(1)}, u32[]{:S(2)}, u32[]{:S(2)}) %collective-permute-start.4) | collective-permute-done | bytes 540704 | tf_op jit(solution)/shard_map/ppermute | solution.py:310
  65.1 0.8 slice.8
  65.9 2.8 %collective-permute-start.7 = (bf16[528,256]{1,0:T(8,128)(2,1)}, bf16[528,256]{1,0:T(8,128)(2,1)S(1)}, u32[]{:S(2)}, u32[]{:S(2)}) collective-permute-start(bf16[528,256]{1,0:T(8,128)(2,1)} %slice.8), channel_id=1, source_target_pairs={{0,2},{1,3},{2,4},{3,5},{4,6},{5,7},{6,0},{7,1},{8,10},{9,11},{10,... | collective-permute-start | bytes 811016 | tf_op jit(solution)/shard_map/ppermute | solution.py:310
  68.7 0.0 collective-permute-done.5.refs_5_
  68.7 0.8 copy-done.3
  69.5 0.7 slice.9
  70.2 0.5 collective-permute-start.8
  70.7 0.6 pad_add_fusion.where_ref
  71.3 5.4 %collective-permute-done.1.refs_1_ = bf16[1056,256]{1,0:T(8,128)(2,1)} collective-permute-done((bf16[1056,256]{1,0:T(8,128)(2,1)S(1)}, bf16[1056,256]{1,0:T(8,128)(2,1)}, u32[]{:S(2)}, u32[]{:S(2)}) %collective-permute-start.1) | collective-permute-done | bytes 540704 | tf_op jit(solution)/shard_map/ppermute | solution.py:310
  76.7 0.0 collective-permute-done.6.refs_6_
  76.7 5.7 %collective-permute-done.7.refs_7_ = bf16[528,256]{1,0:T(8,128)(2,1)S(1)} collective-permute-done((bf16[528,256]{1,0:T(8,128)(2,1)}, bf16[528,256]{1,0:T(8,128)(2,1)S(1)}, u32[]{:S(2)}, u32[]{:S(2)}) %collective-permute-start.7) | collective-permute-done | bytes 270368 | tf_op jit(solution)/shard_map/ppermute | solution.py:310
  82.4 0.0 collective-permute-done.8.refs_8_
  82.4 0.7 copy-done.5
  83.1 1.3 copy-done
  84.5 48.2 %attention.1 = (bf16[512,1024]{1,0:T(8,128)(2,1)}, bf16[512,512]{1,0:T(8,128)(2,1)}) custom-call(s32[3]{0:T(128)} %pad_add_fusion.where_ref, bf16[1056,256]{1,0:T(8,128)(2,1)} %constant_dynamic-update-slice_fusion.after_ref.refs_0_, bf16[1056,256]{1,0:T(8,128)(2,1)} %collective-permute-done.1.refs_1_, bf16[1056,256]{1,0:T(8,128)(2,1)} %collective-permute-done.2.refs_2_, ...), custom_call_target="tpu_custom_call" | custom-call | tf_op jit(solution)/shard_map/attention/pallas_call | solution.py:344
  132.7 1.8 %collective-permute-start.9 = (bf16[512,512]{1,0:T(8,128)(2,1)}, bf16[512,512]{1,0:T(8,128)(2,1)S(1)}, u32[]{:S(2)}, u32[]{:S(2)}) collective-permute-start(bf16[512,512]{1,0:T(8,128)(2,1)} %get-tuple-element.12), channel_id=1, source_target_pairs={{0,1},{1,0},{2,3},{3,2},{4,5},{5,4},{6,7},{7,6},{8,9},{9,8},{10,11... | collective-permute-start | bytes 1572872 | tf_op jit(solution)/shard_map/ppermute | solution.py:313
  134.5 1.7 %collective-permute-done.9 = bf16[512,512]{1,0:T(8,128)(2,1)S(1)} collective-permute-done((bf16[512,512]{1,0:T(8,128)(2,1)}, bf16[512,512]{1,0:T(8,128)(2,1)S(1)}, u32[]{:S(2)}, u32[]{:S(2)}) %collective-permute-start.9) | collective-permute-done | bytes 524320 | tf_op jit(solution)/shard_map/ppermute | solution.py:313
  136.2 0.8 constant_dynamic-update-slice_fusion.1
  (10 shorter events, 0.0 us)
Async XLA Ops:
  3.3 2.1 %collective-permute-start = (bf16[528,256]{1,0:T(8,128)(2,1)}, bf16[528,256]{1,0:T(8,128)(2,1)S(1)}, u32[]{:S(2)}, u32[]{:S(2)}) collective-permute-start(bf16[528,256]{1,0:T(8,128)(2,1)} %get-tuple-element.10), channel_id=1, source_target_pairs={{0,1},{1,0},{2,3},{3,2},{4,5},{5,4},{6,7},{7,6},{8,9},{9,8},{10,11... | collective-permute-start | bytes 811016 | tf_op jit(solution)/shard_map/ppermute | solution.py:313
  10.4 5.8 %copy-start.1 = (bf16[1056,256]{1,0:T(8,128)(2,1)S(1)}, bf16[1056,256]{1,0:T(8,128)(2,1)}, u32[]{:S(2)}) copy-start(bf16[1056,256]{1,0:T(8,128)(2,1)} %constant_dynamic-update-slice_fusion.after_ref.refs_0_) | copy-start | bytes 1622020
  10.4 72.0 %all-to-all-start = ((bf16[16,2,64,512]{3,2,1,0:T(8,128)(2,1)}), bf16[16,2,64,512]{3,2,1,0:T(8,128)(2,1)S(1)}, u32[]{:S(2)}, u32[]{:S(2)}) async-start(bf16[16,2,64,512]{3,2,1,0:T(8,128)(2,1)} %query_projection.1), calls=%async_computation | async-start | bytes 4194304 | tf_op jit(solution)/shard_map/all_to_all | solution.py:332
  16.2 35.9 %collective-permute-start.3 = (bf16[1056,256]{1,0:T(8,128)(2,1)S(1)}, bf16[1056,256]{1,0:T(8,128)(2,1)S(1)}, u32[]{:S(2)}, u32[]{:S(2)}) collective-permute-start(bf16[1056,256]{1,0:T(8,128)(2,1)S(1)} %copy-done.1), channel_id=1, source_target_pairs={{0,8},{1,9},{2,10},{3,11},{4,12},{5,13},{6,14},{7,15},{8,0},{9,1},... | collective-permute-start | bytes 1622024 | tf_op jit(solution)/shard_map/ppermute | solution.py:312
  16.5 36.8 %collective-permute-start.2 = (bf16[1056,256]{1,0:T(8,128)(2,1)S(1)}, bf16[1056,256]{1,0:T(8,128)(2,1)}, u32[]{:S(2)}, u32[]{:S(2)}) collective-permute-start(bf16[1056,256]{1,0:T(8,128)(2,1)S(1)} %copy-done.1), channel_id=1, source_target_pairs={{0,6},{1,7},{2,0},{3,1},{4,2},{5,3},{6,4},{7,5},{8,14},{9,15},{10,... | collective-permute-start | bytes 1622024 | tf_op jit(solution)/shard_map/ppermute | solution.py:311
  52.1 4.8 %copy-start.4 = (bf16[1056,256]{1,0:T(8,128)(2,1)}, bf16[1056,256]{1,0:T(8,128)(2,1)S(1)}, u32[]{:S(2)}) copy-start(bf16[1056,256]{1,0:T(8,128)(2,1)S(1)} %collective-permute-done.3.refs_3_) | copy-start | bytes 1622020
  52.1 13.1 %collective-permute-start.4 = (bf16[1056,256]{1,0:T(8,128)(2,1)S(1)}, bf16[1056,256]{1,0:T(8,128)(2,1)S(1)}, u32[]{:S(2)}, u32[]{:S(2)}) collective-permute-start(bf16[1056,256]{1,0:T(8,128)(2,1)S(1)} %collective-permute-done.3.refs_3_), channel_id=1, source_target_pairs={{0,2},{1,3},{2,4},{3,5},{4,6},{5,7},{6,0},{7,1},{8,10},{9,11},{10,... | collective-permute-start | bytes 1622024 | tf_op jit(solution)/shard_map/ppermute | solution.py:310
  53.3 15.3 %collective-permute-start.5 = (bf16[1056,256]{1,0:T(8,128)(2,1)}, bf16[1056,256]{1,0:T(8,128)(2,1)S(1)}, u32[]{:S(2)}, u32[]{:S(2)}) collective-permute-start(bf16[1056,256]{1,0:T(8,128)(2,1)} %collective-permute-done.2.refs_2_), channel_id=1, source_target_pairs={{0,6},{1,7},{2,0},{3,1},{4,2},{5,3},{6,4},{7,5},{8,14},{9,15},{10,... | collective-permute-start | bytes 1622024 | tf_op jit(solution)/shard_map/ppermute | solution.py:311
  53.5 23.2 %collective-permute-start.1 = (bf16[1056,256]{1,0:T(8,128)(2,1)S(1)}, bf16[1056,256]{1,0:T(8,128)(2,1)}, u32[]{:S(2)}, u32[]{:S(2)}) collective-permute-start(bf16[1056,256]{1,0:T(8,128)(2,1)S(1)} %copy-done.1), channel_id=1, source_target_pairs={{0,2},{1,3},{2,4},{3,5},{4,6},{5,7},{6,0},{7,1},{8,10},{9,11},{10,... | collective-permute-start | bytes 1622024 | tf_op jit(solution)/shard_map/ppermute | solution.py:310
  56.8 19.9 %collective-permute-start.6 = (bf16[1056,256]{1,0:T(8,128)(2,1)}, bf16[1056,256]{1,0:T(8,128)(2,1)}, u32[]{:S(2)}, u32[]{:S(2)}) collective-permute-start(bf16[1056,256]{1,0:T(8,128)(2,1)} %collective-permute-done.2.refs_2_), channel_id=1, source_target_pairs={{0,8},{1,9},{2,10},{3,11},{4,12},{5,13},{6,14},{7,15},{8,0},{9,1},... | collective-permute-start | bytes 1622024 | tf_op jit(solution)/shard_map/ppermute | solution.py:312
  65.1 17.3 %copy-start.2 = (bf16[1056,256]{1,0:T(8,128)(2,1)}, bf16[1056,256]{1,0:T(8,128)(2,1)S(1)}, u32[]{:S(2)}) copy-start(bf16[1056,256]{1,0:T(8,128)(2,1)S(1)} %collective-permute-done.4.refs_4_) | copy-start | bytes 1622020
  65.9 16.5 %collective-permute-start.7 = (bf16[528,256]{1,0:T(8,128)(2,1)}, bf16[528,256]{1,0:T(8,128)(2,1)S(1)}, u32[]{:S(2)}, u32[]{:S(2)}) collective-permute-start(bf16[528,256]{1,0:T(8,128)(2,1)} %slice.8), channel_id=1, source_target_pairs={{0,2},{1,3},{2,4},{3,5},{4,6},{5,7},{6,0},{7,1},{8,10},{9,11},{10,... | collective-permute-start | bytes 811016 | tf_op jit(solution)/shard_map/ppermute | solution.py:310
  68.7 0.8 copy-start.3
  70.2 12.2 %collective-permute-start.8 = (bf16[528,256]{1,0:T(8,128)(2,1)}, bf16[528,256]{1,0:T(8,128)(2,1)}, u32[]{:S(2)}, u32[]{:S(2)}) collective-permute-start(bf16[528,256]{1,0:T(8,128)(2,1)} %slice.9), channel_id=1, source_target_pairs={{0,8},{1,9},{2,10},{3,11},{4,12},{5,13},{6,14},{7,15},{8,0},{9,1},... | collective-permute-start | bytes 811016 | tf_op jit(solution)/shard_map/ppermute | solution.py:312
  82.4 0.7 copy-start.5
  83.1 1.3 copy-start
  132.7 3.6 %collective-permute-start.9 = (bf16[512,512]{1,0:T(8,128)(2,1)}, bf16[512,512]{1,0:T(8,128)(2,1)S(1)}, u32[]{:S(2)}, u32[]{:S(2)}) collective-permute-start(bf16[512,512]{1,0:T(8,128)(2,1)} %get-tuple-element.12), channel_id=1, source_target_pairs={{0,1},{1,0},{2,3},{3,2},{4,5},{5,4},{6,7},{7,6},{8,9},{9,8},{10,11... | collective-permute-start | bytes 1572872 | tf_op jit(solution)/shard_map/ppermute | solution.py:313
